TPU v7x, 32 devices: a whole 2x2x4 slice. The times are simulated.
32 devices in a mesh: src: 16 (over z, y, core), tgt: 2 (over x).
Axes of the slice: x: 2, y: 2, z: 4, core: 2. Of those that a mesh axis runs over, the one named last changes fastest.
Arguments:
- source_mean: float32 [16, 4096], P(None, 'src'), may hold values from -1 to 1, as said below
- target_points: float32 [16, 8192], P(None, 'tgt'), may hold values from -1 to 1
- precision: float32 [16], replicated, may hold values from 0.25 to 2, as said below
- target_values: float32 [8192, 128], P('tgt'), may hold values from 0.5 to 3
- cash: float32 [4096, 128], P('src'), may hold values from -3 to 3
- salvage: float32 [4096, 128], P('src'), may hold values from 0.5 to 3
- switch_cost: float32 [128], replicated, may hold values from 0.05 to 0.5
- cotangent: float32 [4096, 128], P('src'), may hold values from -0.5 to 1.5
- decision: int32 [4096, 128], P('src'), may hold values from 0 to 2
Outputs:
- source_value: float32 [4096, 128], P('src')
- target_adjoint: float32 [2, 4096, 128], P('tgt', 'src')
Inputs may be any that keep to these rules, and one draw needn't show every extreme that they name: `source_mean`: the first factor of source i lies between -1 + 2 i / 4096 and -1 + 2 (i + 1) / 4096. The first factor's precision is 1.5 or more.
All inputs are finite; a program needn't handle non-finite values.
Results may differ from a plain program's by a relative error of at most 0.00024.
Values sent between devices are 32-bit elements; how exact they have to be, the bound alone decides.
No kernel may reach another device: no remote copies, remote signals or barrier semaphores. Data moves between devices by JAX's collectives and lax.ppermute only.
A program may use at most 64 MiB of HBM per device.

v0:
```python
import jax
import jax.numpy as jnp
from jax import lax
from jax.sharding import PartitionSpec as P


def choose_value(continuation, cash_part, salvage_part, cost_part):
    hold_value = continuation + cash_part
    paired = hold_value.reshape(hold_value.shape[0], -1, 2)[:, :, ::-1].reshape(hold_value.shape)
    switched = paired - cost_part[None, :]
    return jnp.maximum(jnp.maximum(hold_value, switched), salvage_part)


def adjoint_input(cotangent, decision):
    held = jnp.where(decision == 0, cotangent, 0.0)
    moved = jnp.where(decision == 1, cotangent, 0.0)
    swapped = moved.reshape(moved.shape[0], -1, 2)[:, :, ::-1].reshape(moved.shape)
    return held + swapped


def transposed_product(left_part, right_part):
    return lax.dot_general(
        left_part,
        right_part,
        (((0,), (0,)), ((), ())),
        precision=lax.Precision.HIGHEST,
        preferred_element_type=jnp.float32,
    )


def on_device(
    source_mean,
    target_points,
    precision,
    target_values,
    cash,
    salvage,
    switch_cost,
    cotangent,
    decision,
):
    source_total = source_mean.shape[1] * lax.axis_size("src")
    target_total = target_points.shape[1] * lax.axis_size("tgt")
    scaled = source_mean * precision[:, None]
    offset = -0.5 * jnp.sum(scaled * source_mean, axis=0)
    density = jnp.exp(transposed_product(scaled, target_points) + offset[:, None])
    column_sum = lax.psum(jnp.sum(density, axis=0), "src")
    factor = source_total / target_total / column_sum
    scaled_values = target_values * factor[:, None]
    partial_terms = jnp.dot(
        density, scaled_values, precision=lax.Precision.HIGHEST, preferred_element_type=jnp.float32
    )
    continuation = lax.psum(partial_terms, "tgt")
    source_value = choose_value(continuation, cash, salvage, switch_cost)
    adjoint_in = adjoint_input(cotangent, decision)
    row_count = target_points.shape[1] // lax.axis_size("src")
    weights = density * factor[None, :]
    weighted_terms = transposed_product(weights, adjoint_in)
    own_rows = lax.psum_scatter(weighted_terms, "src", scatter_dimension=0, tiled=True)
    target_adjoint = own_rows.reshape(1, row_count, own_rows.shape[1])
    return (source_value, target_adjoint)


def solution(mesh):
    placed = (
        P(None, "src"),
        P(None, "tgt"),
        P(),
        P("tgt", None),
        P("src", None),
        P("src", None),
        P(),
        P("src", None),
        P("src", None),
    )
    return jax.shard_map(
        on_device,
        mesh=mesh,
        in_specs=placed,
        out_specs=(P("src", None), P("tgt", "src", None)),
        check_vma=False,
    )
```

profile of v0, /device:TPU:0, one launch (start us, length us, event | category | flops | bytes accessed | tf_op | source)
XLA Modules:
  0.0 162.9 jit_solution(15656077067644059108)
XLA Ops:
  8.0 0.0 copy-start
  8.0 0.0 all-reduce.2.cloned.1.call-start
  8.1 1.0 fusion.13
  9.0 6.3 %fusion.17 = (f32[4096]{0:T(1024)S(1)}, f32[256,4096]{1,0:T(8,128)}) fusion(f32[256]{0:T(256)S(1)} %broadcast_multiply_fusion, f32[16,4096]{1,0:T(8,128)S(1)} %copy-done, f32[16,256]{1,0:T(8,128)} %param.9, f32[16]{0:T(128)} %param.11), kind=kOutput, calls=%fused_computation.23 | convolution fusion | flops 203423744 | bytes 4490304 | tf_op jit(solution)/shard_map/dot_general | solution.py:22
  15.4 63.1 %psum.14 = f32[4096]{0:T(1024)S(1)} all-reduce(f32[4096]{0:T(1024)S(1)} %get-tuple-element.2), channel_id=1, replica_groups=mesh['src'=16,'tgt'=2] {'src'}, use_global_device_ids=true, to_apply=%region_2.0 | all-reduce | flops 4096 | bytes 32768 | tf_op jit(solution)/shard_map/psum | solution.py:47
  78.5 6.4 %fusion.4 = f32[256,128]{1,0:T(8,128)} fusion(f32[256,4096]{1,0:T(8,128)} %get-tuple-element.3, f32[4096,128]{1,0:T(8,128)S(1)} %copy-done.1, f32[4096]{0:T(1024)S(1)} %broadcast_divide_fusion), kind=kOutput, calls=%fused_computation.5 | convolution fusion | flops 1611137024 | bytes 6438912 | tf_op jit(solution)/shard_map/dot_general | solution.py:50
  84.9 0.0 all-reduce.2.cloned.1.call-update
  84.9 0.2 reduce-scatter.2.cloned.1.call-start
  85.1 0.1 copy.14
  85.2 0.1 copy.13
  85.4 0.1 reshape.28
  85.4 0.4 rev.7
  85.8 0.1 reshape.29
  86.0 10.3 %fusion.1 = f32[4096,128]{1,0:T(8,128)} fusion(f32[256,4096]{1,0:T(8,128)} %get-tuple-element.3, f32[4096]{0:T(1024)S(1)} %broadcast_divide_fusion, f32[256,128]{0,1:T(8,128)S(1)} %reshape.29, f32[256,128]{0,1:T(8,128)S(1)} %copy.14, s32[256,128]{0,1:T(8,128)S(1)} %copy.13), kind=kOutput, calls=%fused_computation.2 | convolution fusion | flops 1611759616 | bytes 6701056 | tf_op jit(solution)/shard_map/dot_general | solution.py:22
  96.3 0.0 reduce-scatter.2.cloned.1.call-update
  96.3 7.5 %all-reduce.2.cloned.1.call-done = f32[256,128]{1,0:T(8,128)} async-done(((f32[256,128]{1,0:T(8,128)}), f32[256,128]{1,0:T(8,128)}) %all-reduce.2.cloned.1.call-update) | async-done | bytes 131088 | tf_op jit(solution)/shard_map/psum | solution.py:53
  103.8 0.9 add.22
  104.8 0.1 copy.11
  104.9 0.1 reshape.26
  104.9 0.4 rev.6
  105.3 0.1 reshape.27
  105.4 0.1 copy.12
  105.6 0.7 maximum_maximum_fusion
  106.2 49.2 %reduce-scatter.2.cloned.1.call-done = f32[256,128]{1,0:T(8,128)} async-done(((f32[4096,128]{1,0:T(8,128)}), f32[256,128]{1,0:T(8,128)}) %reduce-scatter.2.cloned.1.call-update) | async-done | bytes 131088 | tf_op jit(solution)/shard_map/reduce_scatter | solution.py:59
  (16 shorter events, 0.1 us)
Async XLA Ops:
  8.0 1.0 copy-start
  8.0 70.5 %copy-start.1 = (f32[4096,128]{1,0:T(8,128)S(1)}, f32[4096,128]{1,0:T(8,128)}, u32[]{:S(2)}) copy-start(f32[4096,128]{1,0:T(8,128)} %param.12) | copy-start | bytes 6291460
  8.0 95.8 %all-reduce.2.cloned.1.call-start = ((), (), s32[]{:S(2)}) async-start(), calls=%async_computation.1 | async-start | bytes 262144 | tf_op jit(solution)/shard_map/psum | solution.py:53
  15.4 69.7 %copy-start.4 = (f32[256,128]{1,0:T(8,128)S(1)}, f32[256,128]{1,0:T(8,128)}, u32[]{:S(2)}) copy-start(f32[256,128]{1,0:T(8,128)} %param.16) | copy-start | bytes 393220
  15.4 69.9 %copy-start.5 = (s32[256,128]{1,0:T(8,128)S(1)}, s32[256,128]{1,0:T(8,128)}, u32[]{:S(2)}) copy-start(s32[256,128]{1,0:T(8,128)} %param.17) | copy-start | bytes 393220
  84.9 70.5 %reduce-scatter.2.cloned.1.call-start = ((), (), s32[]{:S(2)}) async-start(), calls=%async_computation.2 | async-start | bytes 2228224 | tf_op jit(solution)/shard_map/reduce_scatter | solution.py:59
  85.9 17.9 %copy-start.2 = (f32[256,128]{1,0:T(8,128)S(1)}, f32[256,128]{1,0:T(8,128)}, u32[]{:S(2)}) copy-start(f32[256,128]{1,0:T(8,128)} %param.13) | copy-start | bytes 393220
  86.0 19.6 %copy-start.3 = (f32[256,128]{1,0:T(8,128)S(1)}, f32[256,128]{1,0:T(8,128)}, u32[]{:S(2)}) copy-start(f32[256,128]{1,0:T(8,128)} %param.14) | copy-start | bytes 393220
  86.0 19.6 %copy-start.6 = (f32[128]{0:T(128)S(1)}, f32[128]{0:T(128)}, u32[]{:S(2)}) copy-start(f32[128]{0:T(128)} %param.15) | copy-start | bytes 1540
Sparse Core Ops, SparseCore 0:
  85.0 18.7 all-reduce.1
Sparse Core Ops, SparseCore 1:
  96.4 59.0 reduce-scatter.1
where the time goes:
time: 163 us
  blocking collectives  63.1 us (39%)
  waiting for transfers between devices  56.7 us (35%)
  matrix products  23 us (14%)
  between operations  15.6 us (10%)
  other arithmetic  2.59 us (2%)
    psum x1, blocking collectives, on_device(): column_sum = lax.psum(jnp.sum(density, axis=0), 'src')  63.1 us
    reduce_scatter x1, waiting for transfers between devices, on_device(): lax.psum_scatter(weighted_terms, 'src', scatter_dimension=0, tiled=True)  49.2 us
    dot_general x2, matrix products, transposed_product(): lax.dot_general(left_part, right_part, (((0,), (0,)), ((), ())), precisio...  16.6 us
    psum x1, waiting for transfers between devices, on_device(): continuation = lax.psum(partial_terms, 'tgt')  7.53 us
    dot_general x1, matrix products, on_device(): jnp.dot(density, scaled_values, precision=lax.Precision.HIGHEST, preferre...  6.36 us
  transfers between devices with their start and end apart: 2, of which 2 were waited for; matrix products, arithmetic and copies ran while one was open for 8% of the time, Pallas kernels for 0%

commit v1 on v0

v1 whole, which is shorter than its diff:
```python
import math

import jax
import jax.numpy as jnp
from jax import lax
from jax.experimental import pallas as pl
from jax.experimental.pallas import tpu as pltpu
from jax.sharding import PartitionSpec as P

LOG2E = math.log2(math.e)
F32 = jnp.float32
BF16 = jnp.bfloat16


def split2(x):
    hi = x.astype(BF16)
    return hi, (x - hi.astype(F32)).astype(BF16)


def split3(x):
    hi = x.astype(BF16)
    rest = x - hi.astype(F32)
    mid = rest.astype(BF16)
    return hi, mid, (rest - mid.astype(F32)).astype(BF16)


def dot(left, right, left_dim, right_dim):
    return lax.dot_general(left, right, (((left_dim,), (right_dim,)), ((), ())), preferred_element_type=F32)


def source_terms(mean, scale):
    scaled = mean * (scale * LOG2E)
    offset = -0.5 * jnp.sum(scaled * mean, axis=0, keepdims=True)
    s1, s2, s3 = split3(scaled)
    row = lax.broadcasted_iota(jnp.int32, scaled.shape, 0)
    o1, o2, o3 = (jnp.broadcast_to(o.astype(F32), scaled.shape) for o in split3(offset))
    tail = jnp.where(row == 0, o1, jnp.where(row == 1, o2, jnp.where(row == 2, o3, 0.0))).astype(BF16)
    return jnp.concatenate([s1, s1, s2, s2, s1, s3, tail], axis=0)


def target_terms(points):
    t1, t2, t3 = split3(points)
    row = lax.broadcasted_iota(jnp.int32, points.shape, 0)
    tail = jnp.where(row < 3, 1.0, 0.0).astype(BF16)
    return jnp.concatenate([t1, t2, t1, t2, t3, t1, tail], axis=0)


def swap_pairs(x):
    lane = lax.broadcasted_iota(jnp.int32, x.shape, 1)
    width = x.shape[1]
    return jnp.where(lane % 2 == 0, pltpu.roll(x, width - 1, 1), pltpu.roll(x, 1, 1))


def pack_kernel(mean, cotangent, decision, out):
    rows, lanes = cotangent.shape
    held = jnp.where(decision[...] == 0, cotangent[...], 0.0)
    moved = jnp.where(decision[...] == 1, cotangent[...], 0.0)
    out[0:rows, :] = held + swap_pairs(moved)
    factors = mean.shape[0]
    for part in range(mean.shape[1] // lanes):
        out[rows + part * factors : rows + (part + 1) * factors, :] = mean[:, part * lanes : (part + 1) * lanes]


def density_kernel(mean, scale, points, density, column_sum):
    left = source_terms(mean[...], scale[...])
    width = 256
    for j in range(points.shape[1] // width):
        cols = slice(j * width, (j + 1) * width)
        tile = jnp.exp2(dot(left, target_terms(points[:, cols]), 0, 0))
        density[:, cols] = tile
        column_sum[:, cols] = jnp.sum(tile, axis=0, keepdims=True)


def continuation_kernel(density, total, values, out, *, ratio):
    width = 256
    lanes = values.shape[1]
    acc = jnp.zeros((density.shape[0], 2 * lanes), F32)
    low = jnp.zeros((density.shape[0], lanes), F32)
    for j in range(density.shape[1] // width):
        cols = slice(j * width, (j + 1) * width)
        factor = ratio / total[:, cols]
        hi, lo = split2(density[:, cols] * factor)
        vhi, vlo = split2(values[cols, :])
        acc += dot(hi, jnp.concatenate([vhi, vlo], axis=1), 1, 0)
        low += dot(lo, vhi, 1, 0)
    out[...] = acc[:, :lanes] + (acc[:, lanes:] + low)


def adjoint_kernel(scale, points, *refs):
    blocks, out = refs[:-1], refs[-1]
    lanes = out.shape[1]
    factors = points.shape[0]
    rows = out.shape[0]
    step = min(256, rows)
    rights, pairs = [], []
    for block in blocks:
        body = block.shape[0] * lanes // (lanes + factors)
        mean = jnp.concatenate(
            [block[body + p * factors : body + (p + 1) * factors, :] for p in range(body // lanes)], axis=1
        )
        rights.append(source_terms(mean, scale[...]))
        ahi, alo = split2(block[0:body, :])
        pairs.append((jnp.concatenate([ahi, alo], axis=1), ahi))
    for t in range(rows // step):
        left = target_terms(points[:, t * step : (t + 1) * step])
        acc = jnp.zeros((step, 2 * lanes), F32)
        low = jnp.zeros((step, lanes), F32)
        for right, (both, ahi) in zip(rights, pairs):
            hi, lo = split2(jnp.exp2(dot(left, right, 0, 0)))
            acc += dot(hi, both, 1, 0)
            low += dot(lo, ahi, 1, 0)
        out[t * step : (t + 1) * step, :] = acc[:, :lanes] + (acc[:, lanes:] + low)


def value_kernel(own, other, cash, salvage, cost, out):
    hold = own[...] + other[...] + cash[...]
    out[...] = jnp.maximum(jnp.maximum(hold, swap_pairs(hold) - cost[...]), salvage[...])


def call(kernel, out_shape, *args, name):
    return pl.pallas_call(kernel, out_shape=out_shape, name=name)(*args)


def shape(*dims):
    return jax.ShapeDtypeStruct(dims, F32)


def on_device(source_mean, target_points, precision, target_values, cash, salvage, switch_cost, cotangent, decision):
    n = lax.axis_size("src")
    nt = lax.axis_size("tgt")
    factors, sources = source_mean.shape
    targets = target_points.shape[1]
    lanes = cash.shape[1]
    me = lax.axis_index("src")
    scale = precision[:, None]
    ratio = (sources * n) / (targets * nt)
    rows = targets // n
    group = 4

    def flip(x, mask):
        return lax.ppermute(x, "src", [(i, i ^ mask) for i in range(n)])

    packed = call(pack_kernel, shape(sources + factors * sources // lanes, lanes), source_mean, cotangent, decision, name="pack")
    blocks = [packed]
    bit = group
    while bit < n:
        span = min(4, n // bit)
        payload = blocks[0] if len(blocks) == 1 else jnp.stack(blocks)
        received = [flip(payload, k * bit) for k in range(1, span)]
        more = []
        for r in received:
            more += [r] if len(blocks) == 1 else [r[b] for b in range(len(blocks))]
        blocks = blocks + more
        bit *= span

    density, total = call(density_kernel, (shape(sources, targets), shape(1, targets)), source_mean, scale, target_points, name="density")
    mask = 1
    while mask < n:
        total = total + flip(total, mask)
        mask *= 2

    start = (me // group) * (group * rows)
    near_points = lax.dynamic_slice(target_points, (0, start), (factors, group * rows))
    part = call(adjoint_kernel, shape(group * rows, lanes), scale, near_points, *blocks, name="adjoint")
    part = part.reshape(2, 2, rows, lanes)
    core, far = me % 2, (me // 2) % 2
    keep = lax.dynamic_index_in_dim(part, core, 1, keepdims=False)
    send = lax.dynamic_index_in_dim(part, 1 - core, 1, keepdims=False)
    half = keep + flip(send, 1)
    keep = lax.dynamic_index_in_dim(half, far, 0, keepdims=False)
    send = lax.dynamic_index_in_dim(half, 1 - far, 0, keepdims=False)
    own_sum = keep + flip(send, 2)
    own_total = lax.dynamic_slice(total, (0, me * rows), (1, rows))
    target_adjoint = own_sum * (ratio / own_total).reshape(rows, 1)

    def cont(d, t, v, o):
        continuation_kernel(d, t, v, o, ratio=ratio)

    mine = call(cont, shape(sources, lanes), density, total, target_values, name="continuation")
    theirs = mine
    for shift in range(1, nt):
        moved = lax.ppermute(mine, "tgt", [(i, (i + shift) % nt) for i in range(nt)])
        theirs = moved if shift == 1 else theirs + moved
    source_value = call(value_kernel, shape(sources, lanes), mine, theirs, cash, salvage, switch_cost[None, :], name="value")
    return source_value, target_adjoint[None]


def solution(mesh):
    placed = (
        P(None, "src"),
        P(None, "tgt"),
        P(),
        P("tgt", None),
        P("src", None),
        P("src", None),
        P(),
        P("src", None),
        P("src", None),
    )
    return jax.shard_map(
        on_device,
        mesh=mesh,
        in_specs=placed,
        out_specs=(P("src", None), P("tgt", "src", None)),
        check_vma=False,
    )
```

time: 163 us -> 59.8 us (0.37)
  blocking collectives: 63.1 us -> 0 us
  waiting for transfers between devices: 56.7 us -> 17.3 us
  matrix products: 23 us -> 0 us
  Pallas kernels: 0 us -> 17.3 us
  starting transfers between devices: 0.26 us -> 15.4 us
  between operations: 15.6 us -> 0.68 us
  local copies, waits for them, and re-layouts: 1.52 us -> 5.82 us
    psum x1 -> x0, blocking collectives: 63.1 us -> none  [on_device(): column_sum = lax.psum(jnp.sum(density, axis=0), 'src')]
    reduce_scatter x1 -> x0, waiting for transfers between devices: 49.2 us -> none  [on_device(): lax.psum_scatter(weighted_terms, 'src', scatter_dimension=0, tiled=True)]
    dot_general x3 -> x0, matrix products: 23 us -> none  [the longest x2 16.6 us: transposed_product(): lax.dot_general(left_part, right_part, (((0,), (0,)), ((), ())), precisio...]
    pallas_call x0 -> x5, Pallas kernels: none -> 17.3 us  [call(): return pl.pallas_call(kernel, out_shape=out_shape, name=name)(*args)]
    ppermute x0 -> x10, waiting for transfers between devices: none -> 17.3 us  [the longest x9 16 us: flip(): return lax.ppermute(x, 'src', [(i, i ^ mask) for i in range(n)])]
    ppermute x0 -> x10, starting transfers between devices: none -> 15.4 us  [the longest x9 13.9 us: flip(): return lax.ppermute(x, 'src', [(i, i ^ mask) for i in range(n)])]
    psum x1 -> x0, waiting for transfers between devices: 7.53 us -> none  [on_device(): continuation = lax.psum(partial_terms, 'tgt')]
    unnamed x16 -> x10, local copies, waits for them, and re-layouts: 0.23 us -> 1.96 us
  transfers between devices with their start and end apart: 2 -> 10, of which waited for: 2 -> 7; matrix products, arithmetic and copies ran while one was open for 8% -> 8% of each run, Pallas kernels for 0% -> 18%
where the time goes in v1:
time: 59.8 us; the launch traced here: 59.5 us
  Pallas kernels  17.3 us (29%)
  waiting for transfers between devices  17.3 us (29%)
  starting transfers between devices  15.4 us (26%)
  local copies, waits for them, and re-layouts  5.82 us (10%)
  other arithmetic  2.86 us (5%)
  between operations  0.68 us (1%)
    pallas_call x5, Pallas kernels, call(): return pl.pallas_call(kernel, out_shape=out_shape, name=name)(*args)  17.3 us
    ppermute x9, waiting for transfers between devices, flip(): return lax.ppermute(x, 'src', [(i, i ^ mask) for i in range(n)])  16 us
    ppermute x9, starting transfers between devices, flip(): return lax.ppermute(x, 'src', [(i, i ^ mask) for i in range(n)])  13.9 us
    unnamed x10, local copies, waits for them, and re-layouts  1.96 us
    ppermute x1, starting transfers between devices, on_device(): lax.ppermute(mine, 'tgt', [(i, (i + shift) % nt) for i in range(nt)])  1.49 us
    dynamic_slice x1, local copies, waits for them, and re-layouts, on_device(): lax.dynamic_slice(target_points, (0, start), (factors, group * rows))  1.47 us
    add x4, other arithmetic, on_device(): total = total + flip(total, mask)  1.4 us
    ppermute x1, waiting for transfers between devices, on_device(): lax.ppermute(mine, 'tgt', [(i, (i + shift) % nt) for i in range(nt)])  1.36 us
  transfers between devices with their start and end apart: 10, of which 7 were waited for; matrix products, arithmetic and copies ran while one was open for 8% of the time, Pallas kernels for 18%

profile of v1, /device:TPU:0, one launch (start us, length us, event | category | flops | bytes accessed | tf_op | source)
XLA Modules:
  0.0 59.5 jit_solution(6046281733434089543)
XLA Ops:
  0.6 1.8 %pack.1.refs_0_ = f32[288,128]{1,0:T(8,128)} custom-call(f32[16,256]{1,0:T(8,128)} %mean.3, f32[256,128]{1,0:T(8,128)} %cotangent.1, s32[256,128]{1,0:T(8,128)} %decision.1), custom_call_target="tpu_custom_call" | custom-call | tf_op jit(solution)/shard_map/pack/pallas_call | solution.py:121
  2.4 3.1 %collective-permute-start.5 = (f32[288,128]{1,0:T(8,128)}, f32[288,128]{1,0:T(8,128)S(1)}, u32[]{:S(2)}, u32[]{:S(2)}) collective-permute-start(f32[288,128]{1,0:T(8,128)} %pack.1.refs_0_), channel_id=1, source_target_pairs={{0,8},{2,10},{4,12},{6,14},{8,0},{10,2},{12,4},{14,6},{16,24},{18,... | collective-permute-start | bytes 442376 | tf_op jit(solution)/shard_map/ppermute | solution.py:141
  5.5 2.6 %collective-permute-start.6 = (f32[288,128]{1,0:T(8,128)}, f32[288,128]{1,0:T(8,128)S(1)}, u32[]{:S(2)}, u32[]{:S(2)}) collective-permute-start(f32[288,128]{1,0:T(8,128)} %pack.1.refs_0_), channel_id=1, source_target_pairs={{0,16},{2,18},{4,20},{6,22},{8,24},{10,26},{12,28},{14,30},{16,0},... | collective-permute-start | bytes 442376 | tf_op jit(solution)/shard_map/ppermute | solution.py:141
  8.1 1.3 %copy.11.scale = f32[16,1]{1,0:T(8,128)} copy(f32[16,1]{0,1:T(1,128)} %bitcast.21) | data formatting | bytes 128 | tf_op jit(solution)/shard_map/broadcast_in_dim | solution.py:135
  9.4 1.5 %constant_dynamic-slice_fusion.1.points = f32[16,1024]{1,0:T(8,128)} fusion(f32[16,4096]{1,0:T(8,128)} %points.1, s32[]{:T(128)S(6)} %select_n.39), kind=kLoop, calls=%fused_computation.7 | loop fusion | bytes 131076 | tf_op jit(solution)/shard_map/dynamic_slice | solution.py:163
  10.9 0.7 %collective-permute-done.5.refs_1_ = f32[288,128]{1,0:T(8,128)S(1)} collective-permute-done((f32[288,128]{1,0:T(8,128)}, f32[288,128]{1,0:T(8,128)S(1)}, u32[]{:S(2)}, u32[]{:S(2)}) %collective-permute-start.5) | collective-permute-done | bytes 147488 | tf_op jit(solution)/shard_map/ppermute | solution.py:141
  11.6 8.0 %collective-permute-done.6.refs_2_ = f32[288,128]{1,0:T(8,128)S(1)} collective-permute-done((f32[288,128]{1,0:T(8,128)}, f32[288,128]{1,0:T(8,128)S(1)}, u32[]{:S(2)}, u32[]{:S(2)}) %collective-permute-start.6) | collective-permute-done | bytes 147488 | tf_op jit(solution)/shard_map/ppermute | solution.py:141
  20.9 5.1 %adjoint.1 = f32[1024,128]{1,0:T(8,128)} custom-call(f32[16,1]{1,0:T(8,128)} %copy.11.scale, f32[16,1024]{1,0:T(8,128)} %constant_dynamic-slice_fusion.1.points, f32[288,128]{1,0:T(8,128)} %pack.1.refs_0_, f32[288,128]{1,0:T(8,128)} %copy-done.1, f32[288,128]{1,0:T(8,128)} %copy-done.2, f32[288,128]{1,0:T(8,128)} %copy-done.3), custom_call_target="tpu_custom_call" | custom-call | tf_op jit(solution)/shard_map/adjoint/pallas_call | solution.py:121
  26.0 1.0 %dynamic-slice_bitcast_fusion = f32[2,256,128]{2,1,0:T(8,128)S(1)} fusion(f32[2,2,256,128]{3,2,1,0:T(8,128)} %bitcast.18, s32[]{:T(128)S(6)} %select_n.42), kind=kLoop, calls=%fused_computation.1 | loop fusion | bytes 524292 | tf_op jit(solution)/shard_map/jit(dynamic_index_in_dim)/squeeze | solution.py:168
  27.1 3.8 %density.1 = (f32[256,4096]{1,0:T(8,128)}, f32[1,4096]{1,0:T(1,128)}) custom-call(f32[16,256]{1,0:T(8,128)} %mean.3, f32[16,1]{1,0:T(8,128)} %copy.11.scale, f32[16,4096]{1,0:T(8,128)} %points.1), custom_call_target="tpu_custom_call" | custom-call | tf_op jit(solution)/shard_map/density/pallas_call | solution.py:121
  31.4 1.0 %collective-permute-done = f32[1,4096]{1,0:T(1,128)S(1)} collective-permute-done((f32[1,4096]{1,0:T(1,128)}, f32[1,4096]{1,0:T(1,128)S(1)}, u32[]{:S(2)}, u32[]{:S(2)}) %collective-permute-start) | collective-permute-done | bytes 16416 | tf_op jit(solution)/shard_map/ppermute | solution.py:141
  32.5 0.7 %add.49 = f32[1,4096]{1,0:T(1,128)S(1)} add(f32[1,4096]{1,0:T(1,128)} %get-tuple-element.5, f32[1,4096]{1,0:T(1,128)S(1)} %collective-permute-done) | non-fusion elementwise | flops 4096 | bytes 49152 | tf_op jit(solution)/shard_map/add | solution.py:159
  33.2 1.6 %collective-permute-start.1 = (f32[1,4096]{1,0:T(1,128)S(1)}, f32[1,4096]{1,0:T(1,128)S(1)}, u32[]{:S(2)}, u32[]{:S(2)}) collective-permute-start(f32[1,4096]{1,0:T(1,128)S(1)} %add.49), channel_id=1, source_target_pairs={{0,4},{2,6},{4,0},{6,2},{8,12},{10,14},{12,8},{14,10},{16,20},{18,... | collective-permute-start | bytes 49160 | tf_op jit(solution)/shard_map/ppermute | solution.py:141
  34.8 2.2 %collective-permute-done.1 = f32[1,4096]{1,0:T(1,128)S(1)} collective-permute-done((f32[1,4096]{1,0:T(1,128)S(1)}, f32[1,4096]{1,0:T(1,128)S(1)}, u32[]{:S(2)}, u32[]{:S(2)}) %collective-permute-start.1) | collective-permute-done | bytes 16416 | tf_op jit(solution)/shard_map/ppermute | solution.py:141
  37.0 1.8 %collective-permute-start.2 = (f32[1,4096]{1,0:T(1,128)S(1)}, f32[1,4096]{1,0:T(1,128)S(1)}, u32[]{:S(2)}, u32[]{:S(2)}) collective-permute-start(f32[1,4096]{1,0:T(1,128)S(1)} %add.50), channel_id=1, source_target_pairs={{0,8},{2,10},{4,12},{6,14},{8,0},{10,2},{12,4},{14,6},{16,24},{18,... | collective-permute-start | bytes 49160 | tf_op jit(solution)/shard_map/ppermute | solution.py:141
  38.8 2.0 %collective-permute-done.2 = f32[1,4096]{1,0:T(1,128)S(1)} collective-permute-done((f32[1,4096]{1,0:T(1,128)S(1)}, f32[1,4096]{1,0:T(1,128)S(1)}, u32[]{:S(2)}, u32[]{:S(2)}) %collective-permute-start.2) | collective-permute-done | bytes 16416 | tf_op jit(solution)/shard_map/ppermute | solution.py:141
  40.8 2.8 %collective-permute-start.3 = (f32[1,4096]{1,0:T(1,128)S(1)}, f32[1,4096]{1,0:T(1,128)S(1)}, u32[]{:S(2)}, u32[]{:S(2)}) collective-permute-start(f32[1,4096]{1,0:T(1,128)S(1)} %add.51), channel_id=1, source_target_pairs={{0,16},{2,18},{4,20},{6,22},{8,24},{10,26},{12,28},{14,30},{16,0},... | collective-permute-start | bytes 49160 | tf_op jit(solution)/shard_map/ppermute | solution.py:141
  43.6 1.9 %collective-permute-done.3 = f32[1,4096]{1,0:T(1,128)S(1)} collective-permute-done((f32[1,4096]{1,0:T(1,128)S(1)}, f32[1,4096]{1,0:T(1,128)S(1)}, u32[]{:S(2)}, u32[]{:S(2)}) %collective-permute-start.3) | collective-permute-done | bytes 16416 | tf_op jit(solution)/shard_map/ppermute | solution.py:141
  46.2 4.8 %continuation.1.own = f32[256,128]{1,0:T(8,128)} custom-call(f32[256,4096]{1,0:T(8,128)} %get-tuple-element.4.d, f32[1,4096]{1,0:T(1,128)} %add.52.t, f32[4096,128]{1,0:T(8,128)} %v.1), custom_call_target="tpu_custom_call" | custom-call | tf_op jit(solution)/shard_map/continuation/pallas_call | solution.py:121
  51.0 1.5 %collective-permute-start.4 = (f32[256,128]{1,0:T(8,128)}, f32[256,128]{1,0:T(8,128)S(1)}, u32[]{:S(2)}, u32[]{:S(2)}) collective-permute-start(f32[256,128]{1,0:T(8,128)} %continuation.1.own), channel_id=1, source_target_pairs={{0,1},{1,0},{2,3},{3,2},{4,5},{5,4},{6,7},{7,6},{8,9},{9,8},{10,11... | collective-permute-start | bytes 393224 | tf_op jit(solution)/shard_map/ppermute | solution.py:182
  52.5 1.6 %collective-permute-start.9 = (f32[256,128]{1,0:T(8,128)S(1)}, f32[256,128]{1,0:T(8,128)S(1)}, u32[]{:S(2)}, u32[]{:S(2)}) collective-permute-start(f32[256,128]{1,0:T(8,128)S(1)} %dynamic-slice_bitcast_fusion.1), channel_id=1, source_target_pairs={{0,4},{2,6},{4,0},{6,2},{8,12},{10,14},{12,8},{14,10},{16,20},{18,... | collective-permute-start | bytes 393224 | tf_op jit(solution)/shard_map/ppermute | solution.py:141
  54.8 1.4 %collective-permute-done.4.other = f32[256,128]{1,0:T(8,128)S(1)} collective-permute-done((f32[256,128]{1,0:T(8,128)}, f32[256,128]{1,0:T(8,128)S(1)}, u32[]{:S(2)}, u32[]{:S(2)}) %collective-permute-start.4) | collective-permute-done | bytes 131104 | tf_op jit(solution)/shard_map/ppermute | solution.py:182
  56.8 1.9 %value.1 = f32[256,128]{1,0:T(8,128)} custom-call(f32[256,128]{1,0:T(8,128)} %continuation.1.own, f32[256,128]{1,0:T(8,128)} %copy-done.4, f32[256,128]{1,0:T(8,128)} %cash.1, f32[256,128]{1,0:T(8,128)} %salvage.1, f32[1,128]{1,0:T(1,128)} %bitcast.22), custom_call_target="tpu_custom_call" | custom-call | tf_op jit(solution)/shard_map/value/pallas_call | solution.py:121
  58.7 0.8 %fusion.1 = f32[1,256,128]{2,1,0:T(8,128)} fusion(f32[256,128]{1,0:T(8,128)S(1)} %collective-permute-done.9, f32[2,256,128]{2,1,0:T(8,128)S(1)} %bitcast_add_fusion, s32[]{:T(128)S(6)} %select_n.45, f32[256]{0:T(256)S(1)} %bitcast.20), kind=kLoop, calls=%fused_computation.4 | loop fusion | flops 65536 | bytes 394244 | tf_op jit(solution)/shard_map/broadcast_in_dim | solution.py:185
  (22 shorter events, 3.9 us)
Async XLA Ops:
  2.4 9.2 %collective-permute-start.5 = (f32[288,128]{1,0:T(8,128)}, f32[288,128]{1,0:T(8,128)S(1)}, u32[]{:S(2)}, u32[]{:S(2)}) collective-permute-start(f32[288,128]{1,0:T(8,128)} %pack.1.refs_0_), channel_id=1, source_target_pairs={{0,8},{2,10},{4,12},{6,14},{8,0},{10,2},{12,4},{14,6},{16,24},{18,... | collective-permute-start | bytes 442376 | tf_op jit(solution)/shard_map/ppermute | solution.py:141
  5.5 14.1 %collective-permute-start.6 = (f32[288,128]{1,0:T(8,128)}, f32[288,128]{1,0:T(8,128)S(1)}, u32[]{:S(2)}, u32[]{:S(2)}) collective-permute-start(f32[288,128]{1,0:T(8,128)} %pack.1.refs_0_), channel_id=1, source_target_pairs={{0,16},{2,18},{4,20},{6,22},{8,24},{10,26},{12,28},{14,30},{16,0},... | collective-permute-start | bytes 442376 | tf_op jit(solution)/shard_map/ppermute | solution.py:141
  8.1 11.6 %collective-permute-start.7 = (f32[288,128]{1,0:T(8,128)}, f32[288,128]{1,0:T(8,128)S(1)}, u32[]{:S(2)}, u32[]{:S(2)}) collective-permute-start(f32[288,128]{1,0:T(8,128)} %pack.1.refs_0_), channel_id=1, source_target_pairs={{0,24},{2,26},{4,28},{6,30},{8,16},{10,18},{12,20},{14,22},{16,8},... | collective-permute-start | bytes 442376 | tf_op jit(solution)/shard_map/ppermute | solution.py:141
  11.6 8.1 %copy-start.1 = (f32[288,128]{1,0:T(8,128)}, f32[288,128]{1,0:T(8,128)S(1)}, u32[]{:S(2)}) copy-start(f32[288,128]{1,0:T(8,128)S(1)} %collective-permute-done.5.refs_1_) | copy-start | bytes 442372
  19.6 0.7 %copy-start.2 = (f32[288,128]{1,0:T(8,128)}, f32[288,128]{1,0:T(8,128)S(1)}, u32[]{:S(2)}) copy-start(f32[288,128]{1,0:T(8,128)S(1)} %collective-permute-done.6.refs_2_) | copy-start | bytes 442372
  20.3 0.6 %copy-start.3 = (f32[288,128]{1,0:T(8,128)}, f32[288,128]{1,0:T(8,128)S(1)}, u32[]{:S(2)}) copy-start(f32[288,128]{1,0:T(8,128)S(1)} %collective-permute-done.7.refs_3_) | copy-start | bytes 442372
  26.0 26.5 %copy-start = (f32[1024,128]{1,0:T(8,128)S(1)}, f32[1024,128]{1,0:T(8,128)}, u32[]{:S(2)}) copy-start(f32[1024,128]{1,0:T(8,128)} %adjoint.1) | copy-start | bytes 1572868
  27.1 25.4 %collective-permute-start.8 = (f32[2,256,128]{2,1,0:T(8,128)S(1)}, f32[2,256,128]{2,1,0:T(8,128)S(1)}, u32[]{:S(2)}, u32[]{:S(2)}) collective-permute-start(f32[2,256,128]{2,1,0:T(8,128)S(1)} %dynamic-slice_bitcast_fusion), channel_id=1, source_target_pairs={{0,2},{2,0},{4,6},{6,4},{8,10},{10,8},{12,14},{14,12},{16,18},{18,... | collective-permute-start | bytes 786440 | tf_op jit(solution)/shard_map/ppermute | solution.py:141
  30.9 1.5 %collective-permute-start = (f32[1,4096]{1,0:T(1,128)}, f32[1,4096]{1,0:T(1,128)S(1)}, u32[]{:S(2)}, u32[]{:S(2)}) collective-permute-start(f32[1,4096]{1,0:T(1,128)} %get-tuple-element.5), channel_id=1, source_target_pairs={{0,2},{2,0},{4,6},{6,4},{8,10},{10,8},{12,14},{14,12},{16,18},{18,... | collective-permute-start | bytes 49160 | tf_op jit(solution)/shard_map/ppermute | solution.py:141
  33.2 3.8 %collective-permute-start.1 = (f32[1,4096]{1,0:T(1,128)S(1)}, f32[1,4096]{1,0:T(1,128)S(1)}, u32[]{:S(2)}, u32[]{:S(2)}) collective-permute-start(f32[1,4096]{1,0:T(1,128)S(1)} %add.49), channel_id=1, source_target_pairs={{0,4},{2,6},{4,0},{6,2},{8,12},{10,14},{12,8},{14,10},{16,20},{18,... | collective-permute-start | bytes 49160 | tf_op jit(solution)/shard_map/ppermute | solution.py:141
  37.0 3.8 %collective-permute-start.2 = (f32[1,4096]{1,0:T(1,128)S(1)}, f32[1,4096]{1,0:T(1,128)S(1)}, u32[]{:S(2)}, u32[]{:S(2)}) collective-permute-start(f32[1,4096]{1,0:T(1,128)S(1)} %add.50), channel_id=1, source_target_pairs={{0,8},{2,10},{4,12},{6,14},{8,0},{10,2},{12,4},{14,6},{16,24},{18,... | collective-permute-start | bytes 49160 | tf_op jit(solution)/shard_map/ppermute | solution.py:141
  40.8 4.7 %collective-permute-start.3 = (f32[1,4096]{1,0:T(1,128)S(1)}, f32[1,4096]{1,0:T(1,128)S(1)}, u32[]{:S(2)}, u32[]{:S(2)}) collective-permute-start(f32[1,4096]{1,0:T(1,128)S(1)} %add.51), channel_id=1, source_target_pairs={{0,16},{2,18},{4,20},{6,22},{8,24},{10,26},{12,28},{14,30},{16,0},... | collective-permute-start | bytes 49160 | tf_op jit(solution)/shard_map/ppermute | solution.py:141
  51.0 5.2 %collective-permute-start.4 = (f32[256,128]{1,0:T(8,128)}, f32[256,128]{1,0:T(8,128)S(1)}, u32[]{:S(2)}, u32[]{:S(2)}) collective-permute-start(f32[256,128]{1,0:T(8,128)} %continuation.1.own), channel_id=1, source_target_pairs={{0,1},{1,0},{2,3},{3,2},{4,5},{5,4},{6,7},{7,6},{8,9},{9,8},{10,11... | collective-permute-start | bytes 393224 | tf_op jit(solution)/shard_map/ppermute | solution.py:182
  52.5 6.2 %collective-permute-start.9 = (f32[256,128]{1,0:T(8,128)S(1)}, f32[256,128]{1,0:T(8,128)S(1)}, u32[]{:S(2)}, u32[]{:S(2)}) collective-permute-start(f32[256,128]{1,0:T(8,128)S(1)} %dynamic-slice_bitcast_fusion.1), channel_id=1, source_target_pairs={{0,4},{2,6},{4,0},{6,2},{8,12},{10,14},{12,8},{14,10},{16,20},{18,... | collective-permute-start | bytes 393224 | tf_op jit(solution)/shard_map/ppermute | solution.py:141
  56.1 0.7 %copy-start.4 = (f32[256,128]{1,0:T(8,128)}, f32[256,128]{1,0:T(8,128)S(1)}, u32[]{:S(2)}) copy-start(f32[256,128]{1,0:T(8,128)S(1)} %collective-permute-done.4.other) | copy-start | bytes 393220

commit v2 on v1

v2 whole, which is shorter than its diff:
```python
import math

import jax
import jax.numpy as jnp
from jax import lax
from jax.experimental import pallas as pl
from jax.experimental.pallas import tpu as pltpu
from jax.sharding import PartitionSpec as P


LOG2E = math.log2(math.e)
F32 = jnp.float32
BF16 = jnp.bfloat16
GRANT = 16 * 2**20


def split2(x):
    hi = x.astype(BF16)
    return hi, (x - hi.astype(F32)).astype(BF16)


def split3(x):
    hi = x.astype(BF16)
    rest = x - hi.astype(F32)
    mid = rest.astype(BF16)
    return hi, mid, (rest - mid.astype(F32)).astype(BF16)


def dot(left, right, left_dim, right_dim):
    return lax.dot_general(left, right, (((left_dim,), (right_dim,)), ((), ())), preferred_element_type=F32)


def source_terms(mean, scale):
    scaled = mean * scale
    offset = -0.5 * jnp.sum(scaled * mean, axis=0, keepdims=True)
    s1, s2, s3 = split3(scaled)
    row = lax.broadcasted_iota(jnp.int32, scaled.shape, 0)
    o1, o2, o3 = (jnp.broadcast_to(o.astype(F32), scaled.shape) for o in split3(offset))
    tail = jnp.where(row == 0, o1, jnp.where(row == 1, o2, jnp.where(row == 2, o3, 0.0))).astype(BF16)
    return jnp.concatenate([s1, s1, s2, s2, s1, s3, tail], axis=0)


def target_terms(points):
    t1, t2, t3 = split3(points)
    row = lax.broadcasted_iota(jnp.int32, points.shape, 0)
    tail = jnp.where(row < 3, 1.0, 0.0).astype(BF16)
    return jnp.concatenate([t1, t2, t1, t2, t3, t1, tail], axis=0)


def swap_pairs(x):
    lane = lax.broadcasted_iota(jnp.int32, x.shape, 1)
    width = x.shape[1]
    return jnp.where(lane % 2 == 0, pltpu.roll(x, width - 1, 1), pltpu.roll(x, 1, 1))


def column(row):
    n = row.shape[1]
    wide = jnp.broadcast_to(row, (n, n))
    diagonal = lax.broadcasted_iota(jnp.int32, (n, n), 0) == lax.broadcasted_iota(jnp.int32, (n, n), 1)
    return jnp.sum(jnp.where(diagonal, wide, 0.0), axis=1, keepdims=True)


def pack_kernel(mean, cotangent, decision, out):
    rows, lanes = cotangent.shape
    held = jnp.where(decision[...] == 0, cotangent[...], 0.0)
    moved = jnp.where(decision[...] == 1, cotangent[...], 0.0)
    out[0:rows, :] = held + swap_pairs(moved)
    factors = mean.shape[0]
    for part in range(mean.shape[1] // lanes):
        out[rows + part * factors : rows + (part + 1) * factors, :] = mean[:, part * lanes : (part + 1) * lanes]


def own_kernel(mean, precision, points, scale_out, terms_out, total_out):
    scale = column(precision[...]) * LOG2E
    scale_out[...] = jnp.broadcast_to(scale, scale_out.shape)
    left = source_terms(mean[...], scale)
    width = 256
    for j in range(points.shape[1] // width):
        cols = slice(j * width, (j + 1) * width)
        terms = target_terms(points[:, cols])
        terms_out[:, cols] = terms
        total_out[:, cols] = jnp.sum(jnp.exp2(dot(left, terms, 0, 0)), axis=0, keepdims=True)


def unpack_mean(block, factors):
    lanes = block.shape[1]
    body = block.shape[0] * lanes // (lanes + factors)
    return body, jnp.concatenate(
        [block[body + p * factors : body + (p + 1) * factors, :] for p in range(body // lanes)], axis=1
    )


def total_kernel(scale, terms, total, *refs):
    blocks, out = refs[:-1], refs[-1]
    lefts = [source_terms(unpack_mean(block, scale.shape[0])[1], scale[:, :1]) for block in blocks]
    width = 256
    for j in range(terms.shape[1] // width):
        cols = slice(j * width, (j + 1) * width)
        tile = sum(jnp.exp2(dot(left, terms[:, cols], 0, 0)) for left in lefts)
        out[:, cols] = total[:, cols] + jnp.sum(tile, axis=0, keepdims=True)


def continuation_kernel(mean, scale, terms, total, arrived, values, out, *, ratio):
    width = 256
    lanes = values.shape[1]
    left = source_terms(mean[...], scale[:, :1])
    acc = jnp.zeros((mean.shape[1], 2 * lanes), F32)
    low = jnp.zeros((mean.shape[1], lanes), F32)
    for j in range(terms.shape[1] // width):
        cols = slice(j * width, (j + 1) * width)
        factor = ratio / (total[:, cols] + arrived[:, cols])
        hi, lo = split2(jnp.exp2(dot(left, terms[:, cols], 0, 0)) * factor)
        vhi, vlo = split2(values[cols, :])
        acc += dot(hi, jnp.concatenate([vhi, vlo], axis=1), 1, 0)
        low += dot(lo, vhi, 1, 0)
    out[...] = acc[:, :lanes] + (acc[:, lanes:] + low)


def adjoint_kernel(where, scale, terms, *refs, masks):
    blocks, out = refs[:-1], refs[-1]
    lanes = out.shape[-1]
    rows = out.shape[1]
    rights, pairs = [], []
    for block in blocks:
        body, mean = unpack_mean(block, scale.shape[0])
        rights.append(source_terms(mean, scale[:, :1]))
        ahi, alo = split2(block[0:body, :])
        pairs.append((jnp.concatenate([ahi, alo], axis=1), ahi))
    for slot, mask in enumerate(masks):
        if rows % 128 == 0:
            start = pl.multiple_of((where[0] ^ mask) * rows, 128)
        else:
            start = slot * rows
        left = terms[:, pl.ds(start, rows)]
        acc = jnp.zeros((rows, 2 * lanes), F32)
        low = jnp.zeros((rows, lanes), F32)
        for right, (both, ahi) in zip(rights, pairs):
            hi, lo = split2(jnp.exp2(dot(left, right, 0, 0)))
            acc += dot(hi, both, 1, 0)
            low += dot(lo, ahi, 1, 0)
        out[slot] = acc[:, :lanes] + (acc[:, lanes:] + low)


def value_kernel(own, other, cash, salvage, cost, out):
    hold = own[...] + other[...] + cash[...]
    out[...] = jnp.maximum(jnp.maximum(hold, swap_pairs(hold) - cost[...]), salvage[...])


def finish_kernel(own, other, total, out, *, ratio):
    factor = column(ratio / total[...])
    out[...] = (own[...] + other[...]) * factor


def call(kernel, out_shape, *args):
    vmem = pl.BlockSpec(memory_space=pltpu.VMEM)
    smem = pl.BlockSpec(memory_space=pltpu.SMEM)
    specs, operands = [], []
    for a in args:
        if isinstance(a, Far):
            specs.append(vmem)
            operands.append(a.array)
        elif a.shape == (1,):
            specs.append(smem)
            operands.append(a)
        else:
            specs.append(vmem)
            operands.append(pltpu.with_memory_space_constraint(a, pltpu.VMEM))
    return pl.pallas_call(
        kernel,
        out_shape=out_shape,
        in_specs=specs,
        out_specs=jax.tree.map(lambda _: vmem, out_shape),
        compiler_params=pltpu.CompilerParams(vmem_limit_bytes=GRANT),
    )(*operands)


class Far:
    def __init__(self, array):
        self.array = array


def shape(*dims, dtype=F32):
    return pltpu.VMEM(dims, dtype)


def result(*dims):
    return jax.ShapeDtypeStruct(dims, F32)


def on_device(source_mean, target_points, precision, target_values, cash, salvage, switch_cost, cotangent, decision):
    n = lax.axis_size("src")
    nt = lax.axis_size("tgt")
    factors, sources = source_mean.shape
    targets = target_points.shape[1]
    lanes = cash.shape[1]
    me = lax.axis_index("src")
    where = me[None].astype(jnp.int32)
    ratio = (sources * n) / (targets * nt)
    rows = targets // n
    top = n // 2

    def flip(x, mask):
        return lax.ppermute(x, "src", [(i, i ^ mask) for i in range(n)])

    packed = call(
        pack_kernel, shape(sources + factors * sources // lanes, lanes), Far(source_mean), Far(cotangent), Far(decision)
    )
    groups = []
    blocks = [packed]
    bit, level = 2, 0
    while bit < top:
        span = min(4, top // bit)
        payload = blocks[0] if len(blocks) == 1 else jnp.stack(blocks)
        more = []
        for k in reversed(range(1, span)):
            r = flip(payload, k * bit)
            more.append([r] if len(blocks) == 1 else [r[b] for b in range(len(blocks))])
        if level == 0:
            groups += [[b for g in more[1:] for b in g], more[0]]
        else:
            groups += more
        blocks = blocks + [b for g in more for b in g]
        bit *= span
        level += 1

    scale, terms, total = call(
        own_kernel,
        (shape(factors, lanes), shape(7 * factors, targets, dtype=BF16), shape(1, targets)),
        Far(source_mean),
        Far(precision[None, :]),
        Far(target_points),
    )
    for group in groups:
        total = call(total_kernel, shape(1, targets), scale, terms, total, *group)
    total = total + flip(total, 1)
    arrived = flip(total, top)

    def adjoint(masks):
        if rows % 128 == 0:
            near = terms
        else:
            near = jnp.concatenate(
                [lax.dynamic_slice(terms, (0, (me ^ mask) * rows), (terms.shape[0], rows)) for mask in masks], axis=1
            )

        def kernel(*refs):
            adjoint_kernel(*refs, masks=masks)

        return call(kernel, shape(len(masks), rows, lanes), where, scale, near, *blocks)

    away = adjoint((1, 1 ^ top))
    came = flip(away, 1)
    near = adjoint((0, top))
    far_half = near[1] + came[1]
    came_far = flip(far_half, top)
    own_half = near[0] + came[0]
    own_total = lax.dynamic_slice(total, (0, me * rows), (1, rows)) + lax.dynamic_slice(arrived, (0, me * rows), (1, rows))

    def finish(a, b, t, o):
        finish_kernel(a, b, t, o, ratio=ratio)

    target_adjoint = call(finish, result(rows, lanes), own_half, came_far, own_total)

    def cont(*refs):
        continuation_kernel(*refs, ratio=ratio)

    mine = call(cont, shape(sources, lanes), source_mean, scale, terms, total, arrived, target_values)
    theirs = mine
    for shift in range(1, nt):
        moved = lax.ppermute(mine, "tgt", [(i, (i + shift) % nt) for i in range(nt)])
        theirs = moved if shift == 1 else theirs + moved
    source_value = call(value_kernel, result(sources, lanes), mine, theirs, cash, salvage, switch_cost[None, :])
    return source_value, target_adjoint[None]


def solution(mesh):
    placed = (
        P(None, "src"),
        P(None, "tgt"),
        P(),
        P("tgt", None),
        P("src", None),
        P("src", None),
        P(),
        P("src", None),
        P("src", None),
    )

    return jax.shard_map(
        on_device,
        mesh=mesh,
        in_specs=placed,
        out_specs=(P("src", None), P("tgt", "src", None)),
        check_vma=False,
    )
```

time: 59.8 us -> 40 us (0.67)
  waiting for transfers between devices: 17.3 us -> 10.3 us
  Pallas kernels: 17.3 us -> 11.7 us
  starting transfers between devices: 15.4 us -> 12 us
  other arithmetic: 2.86 us -> 0.06 us
  local copies, waits for them, and re-layouts: 5.82 us -> 4.87 us
    ppermute x9 -> x7, waiting for transfers between devices: 16 us -> 9.33 us  [flip(): return lax.ppermute(x, 'src', [(i, i ^ mask) for i in range(n)])]
    pallas_call x5 -> x9, Pallas kernels: 17.3 us -> 11.7 us  [call(): pl.pallas_call(kernel, out_shape=out_shape, in_specs=specs, out_specs=jax...]
    ppermute x9 -> x7, starting transfers between devices: 13.9 us -> 10.4 us  [flip(): return lax.ppermute(x, 'src', [(i, i ^ mask) for i in range(n)])]
    unnamed x10 -> x20, local copies, waits for them, and re-layouts: 1.96 us -> 4.87 us
    dynamic_slice x1 -> x0, local copies, waits for them, and re-layouts: 1.47 us -> none  [on_device(): lax.dynamic_slice(target_points, (0, start), (factors, group * rows))]
    add x5 -> x3, other arithmetic: 1.42 us -> 0.06 us  [the longest x1 0.03 us: on_device(): far_half = near[1] + came[1]]
    broadcast_in_dim x1 -> x0, local copies, waits for them, and re-layouts: 1.33 us -> none  [on_device(): scale = precision[:, None]]
    squeeze x2 -> x0, local copies, waits for them, and re-layouts: 1.06 us -> none  [the longest x1 1.04 us: on_device(): send = lax.dynamic_index_in_dim(part, 1 - core, 1, keepdims=False)]
  transfers between devices with their start and end apart: 10 -> 8, of which waited for: 7 -> 5; matrix products, arithmetic and copies ran while one was open for 8% -> 0% of each run, Pallas kernels for 18% -> 23%
where the time goes in v2:
time: 40 us; the launch traced here: 39.6 us
  starting transfers between devices  12 us (30%)
  Pallas kernels  11.7 us (29%)
  waiting for transfers between devices  10.3 us (26%)
  local copies, waits for them, and re-layouts  4.87 us (12%)
  between operations  0.75 us (2%)
    pallas_call x9, Pallas kernels, call(): pl.pallas_call(kernel, out_shape=out_shape, in_specs=specs, out_specs=jax...  11.7 us
    ppermute x7, starting transfers between devices, flip(): return lax.ppermute(x, 'src', [(i, i ^ mask) for i in range(n)])  10.4 us
    ppermute x7, waiting for transfers between devices, flip(): return lax.ppermute(x, 'src', [(i, i ^ mask) for i in range(n)])  9.33 us
    unnamed x20, local copies, waits for them, and re-layouts  4.87 us
    ppermute x1, starting transfers between devices, on_device(): lax.ppermute(mine, 'tgt', [(i, (i + shift) % nt) for i in range(nt)])  1.55 us
    ppermute x1, waiting for transfers between devices, on_device(): lax.ppermute(mine, 'tgt', [(i, (i + shift) % nt) for i in range(nt)])  0.95 us
  transfers between devices with their start and end apart: 8, of which 5 were waited for; matrix products, arithmetic and copies ran while one was open for 0% of the time, Pallas kernels for 23%

profile of v2, /device:TPU:0, one launch (start us, length us, event | category | flops | bytes accessed | tf_op | source)
XLA Modules:
  0.0 39.6 jit_solution(7053790501904846733)
XLA Ops:
  0.6 0.7 %copy-done.2 = f32[16,256]{1,0:T(8,128)S(1)} copy-done((f32[16,256]{1,0:T(8,128)S(1)}, f32[16,256]{1,0:T(8,128)}, u32[]{:S(2)}) %copy-start.2) | copy-done | bytes 16408
  1.4 0.9 %copy-done.4 = f32[256,128]{1,0:T(8,128)S(1)} copy-done((f32[256,128]{1,0:T(8,128)S(1)}, f32[256,128]{1,0:T(8,128)}, u32[]{:S(2)}) %copy-start.4) | copy-done | bytes 131096
  2.3 0.9 %copy-done.5 = s32[256,128]{1,0:T(8,128)S(1)} copy-done((s32[256,128]{1,0:T(8,128)S(1)}, s32[256,128]{1,0:T(8,128)}, u32[]{:S(2)}) %copy-start.5) | copy-done | bytes 131096
  3.3 3.1 %collective-permute-start = (f32[288,128]{1,0:T(8,128)S(1)}, f32[288,128]{1,0:T(8,128)S(1)}, u32[]{:S(2)}, u32[]{:S(2)}) collective-permute-start(f32[288,128]{1,0:T(8,128)S(1)} %shard_map.105.refs_3_), channel_id=1, source_target_pairs={{0,8},{2,10},{4,12},{6,14},{8,0},{10,2},{12,4},{14,6},{16,24},{18,... | collective-permute-start | bytes 442376 | tf_op jit(solution)/shard_map/ppermute | solution.py:203
  6.4 1.5 %collective-permute-start.1 = (f32[288,128]{1,0:T(8,128)S(1)}, f32[288,128]{1,0:T(8,128)S(1)}, u32[]{:S(2)}, u32[]{:S(2)}) collective-permute-start(f32[288,128]{1,0:T(8,128)S(1)} %shard_map.105.refs_3_), channel_id=1, source_target_pairs={{0,4},{2,6},{4,0},{6,2},{8,12},{10,14},{12,8},{14,10},{16,20},{18,... | collective-permute-start | bytes 442376 | tf_op jit(solution)/shard_map/ppermute | solution.py:203
  8.0 0.9 %copy-done.1 = f32[16,4096]{1,0:T(8,128)S(1)} copy-done((f32[16,4096]{1,0:T(8,128)S(1)}, f32[16,4096]{1,0:T(8,128)}, u32[]{:S(2)}) %copy-start.1) | copy-done | bytes 262168
  8.9 0.7 %copy-done.3 = f32[16,256]{1,0:T(8,128)S(1)} copy-done((f32[16,256]{1,0:T(8,128)S(1)}, f32[16,256]{1,0:T(8,128)}, u32[]{:S(2)}) %copy-start.3) | copy-done | bytes 16408
  9.6 0.7 %copy-done.8 = f32[16]{0:T(128)S(1)} copy-done((f32[16]{0:T(128)S(1)}, f32[16]{0:T(128)}, u32[]{:S(2)}) %copy-start.8) | copy-done | bytes 88
  10.3 0.8 %shard_map.104 = (f32[16,128]{1,0:T(8,128)S(1)}, bf16[112,4096]{1,0:T(8,128)(2,1)S(1)}, f32[1,4096]{1,0:T(1,128)S(1)}) custom-call(f32[16,256]{1,0:T(8,128)S(1)} %copy-done.3, f32[1,16]{1,0:T(1,128)S(1)} %bitcast.8, f32[16,4096]{1,0:T(8,128)S(1)} %copy-done.1), custom_call_target="tpu_custom_call" | custom-call | tf_op jit(solution)/shard_map/pallas_call | solution.py:168
  11.1 3.8 %collective-permute-done.1.refs_1_.refs_6_ = f32[288,128]{1,0:T(8,128)S(1)} collective-permute-done((f32[288,128]{1,0:T(8,128)S(1)}, f32[288,128]{1,0:T(8,128)S(1)}, u32[]{:S(2)}, u32[]{:S(2)}) %collective-permute-start.1) | collective-permute-done | bytes 147488 | tf_op jit(solution)/shard_map/ppermute | solution.py:203
  14.9 1.7 %shard_map.111 = f32[2,256,128]{2,1,0:T(8,128)S(1)} custom-call(s32[1]{0:T(128)} %bitcast.2.refs_0_, f32[16,128]{1,0:T(8,128)S(1)} %get-tuple-element.5.scale.refs_1_, bf16[112,4096]{1,0:T(8,128)(2,1)S(1)} %get-tuple-element.6.terms.refs_2_, f32[288,128]{1,0:T(8,128)S(1)} %shard_map.105.refs_3_, f32[288,128]{1,0:T(8,128)S(1)} %collective-permute-done.2.refs_0_.refs_4_, ...), custom_call_target="tpu_custom_call" | custom-call | tf_op jit(solution)/shard_map/pallas_call | solution.py:168
  16.6 1.4 %shard_map.106.total = f32[1,4096]{1,0:T(1,128)S(1)} custom-call(f32[16,128]{1,0:T(8,128)S(1)} %get-tuple-element.5.scale.refs_1_, bf16[112,4096]{1,0:T(8,128)(2,1)S(1)} %get-tuple-element.6.terms.refs_2_, f32[1,4096]{1,0:T(1,128)S(1)} %get-tuple-element.7.total, f32[288,128]{1,0:T(8,128)S(1)} %collective-permute-done.refs_0_.refs_5_, ...), custom_call_target="tpu_custom_call" | custom-call | tf_op jit(solution)/shard_map/pallas_call | solution.py:168
  18.0 0.8 %shard_map.107 = f32[1,4096]{1,0:T(1,128)S(1)} custom-call(f32[16,128]{1,0:T(8,128)S(1)} %get-tuple-element.5.scale.refs_1_, bf16[112,4096]{1,0:T(8,128)(2,1)S(1)} %get-tuple-element.6.terms.refs_2_, f32[1,4096]{1,0:T(1,128)S(1)} %shard_map.106.total, f32[288,128]{1,0:T(8,128)S(1)} %collective-permute-done.2.refs_0_.refs_4_), custom_call_target="tpu_custom_call" | custom-call | tf_op jit(solution)/shard_map/pallas_call | solution.py:168
  18.9 0.6 %collective-permute-start.3 = (f32[1,4096]{1,0:T(1,128)S(1)}, f32[1,4096]{1,0:T(1,128)S(1)}, u32[]{:S(2)}, u32[]{:S(2)}) collective-permute-start(f32[1,4096]{1,0:T(1,128)S(1)} %shard_map.107), channel_id=1, source_target_pairs={{0,2},{2,0},{4,6},{6,4},{8,10},{10,8},{12,14},{14,12},{16,18},{18,... | collective-permute-start | bytes 49160 | tf_op jit(solution)/shard_map/ppermute | solution.py:203
  19.4 0.8 %collective-permute-done.3 = f32[1,4096]{1,0:T(1,128)S(1)} collective-permute-done((f32[1,4096]{1,0:T(1,128)S(1)}, f32[1,4096]{1,0:T(1,128)S(1)}, u32[]{:S(2)}, u32[]{:S(2)}) %collective-permute-start.3) | collective-permute-done | bytes 16416 | tf_op jit(solution)/shard_map/ppermute | solution.py:203
  20.3 2.7 %collective-permute-start.4 = (f32[1,4096]{1,0:T(1,128)S(1)}, f32[1,4096]{1,0:T(1,128)S(1)}, u32[]{:S(2)}, u32[]{:S(2)}) collective-permute-start(f32[1,4096]{1,0:T(1,128)S(1)} %add.21.refs_3_), channel_id=1, source_target_pairs={{0,16},{2,18},{4,20},{6,22},{8,24},{10,26},{12,28},{14,30},{16,0},... | collective-permute-start | bytes 49160 | tf_op jit(solution)/shard_map/ppermute | solution.py:203
  22.9 1.7 %shard_map.110 = f32[2,256,128]{2,1,0:T(8,128)S(1)} custom-call(s32[1]{0:T(128)} %bitcast.2.refs_0_, f32[16,128]{1,0:T(8,128)S(1)} %get-tuple-element.5.scale.refs_1_, bf16[112,4096]{1,0:T(8,128)(2,1)S(1)} %get-tuple-element.6.terms.refs_2_, f32[288,128]{1,0:T(8,128)S(1)} %shard_map.105.refs_3_, f32[288,128]{1,0:T(8,128)S(1)} %collective-permute-done.2.refs_0_.refs_4_, ...), custom_call_target="tpu_custom_call" | custom-call | tf_op jit(solution)/shard_map/pallas_call | solution.py:168
  25.2 3.6 %shard_map.108.own = f32[256,128]{1,0:T(8,128)S(1)} custom-call(f32[16,256]{1,0:T(8,128)S(1)} %copy-done.3, f32[16,128]{1,0:T(8,128)S(1)} %get-tuple-element.5.scale.refs_1_, bf16[112,4096]{1,0:T(8,128)(2,1)S(1)} %get-tuple-element.6.terms.refs_2_, f32[1,4096]{1,0:T(1,128)S(1)} %add.21.refs_3_, f32[1,4096]{1,0:T(1,128)S(1)} %collective-permute-done.4.refs_4_, ...), custom_call_target="tpu_custom_call" | custom-call | tf_op jit(solution)/shard_map/pallas_call | solution.py:168
  28.8 1.6 %collective-permute-start.5 = (f32[256,128]{1,0:T(8,128)S(1)}, f32[256,128]{1,0:T(8,128)S(1)}, u32[]{:S(2)}, u32[]{:S(2)}) collective-permute-start(f32[256,128]{1,0:T(8,128)S(1)} %shard_map.108.own), channel_id=1, source_target_pairs={{0,1},{1,0},{2,3},{3,2},{4,5},{5,4},{6,7},{7,6},{8,9},{9,8},{10,11... | collective-permute-start | bytes 393224 | tf_op jit(solution)/shard_map/ppermute | solution.py:270
  30.4 2.5 %collective-permute-start.7 = (f32[256,128]{1,0:T(8,128)S(1)}, f32[256,128]{1,0:T(8,128)S(1)}, u32[]{:S(2)}, u32[]{:S(2)}) collective-permute-start(f32[256,128]{1,0:T(8,128)S(1)} %get-tuple-element.8), channel_id=1, source_target_pairs={{0,16},{2,18},{4,20},{6,22},{8,24},{10,26},{12,28},{14,30},{16,0},... | collective-permute-start | bytes 393224 | tf_op jit(solution)/shard_map/ppermute | solution.py:203
  32.9 1.0 %collective-permute-done.5.other = f32[256,128]{1,0:T(8,128)S(1)} collective-permute-done((f32[256,128]{1,0:T(8,128)S(1)}, f32[256,128]{1,0:T(8,128)S(1)}, u32[]{:S(2)}, u32[]{:S(2)}) %collective-permute-start.5) | collective-permute-done | bytes 131104 | tf_op jit(solution)/shard_map/ppermute | solution.py:270
  33.8 0.8 %shard_map.109 = f32[256,128]{1,0:T(8,128)} custom-call(f32[256,128]{1,0:T(8,128)S(1)} %shard_map.108.own, f32[256,128]{1,0:T(8,128)S(1)} %collective-permute-done.5.other, f32[256,128]{1,0:T(8,128)S(1)} %copy-done.6, f32[256,128]{1,0:T(8,128)S(1)} %copy-done.7, f32[1,128]{1,0:T(1,128)S(1)} %bitcast.9), custom_call_target="tpu_custom_call" | custom-call | tf_op jit(solution)/shard_map/pallas_call | solution.py:168
  34.6 4.2 %collective-permute-done.7.b = f32[256,128]{1,0:T(8,128)S(1)} collective-permute-done((f32[256,128]{1,0:T(8,128)S(1)}, f32[256,128]{1,0:T(8,128)S(1)}, u32[]{:S(2)}, u32[]{:S(2)}) %collective-permute-start.7) | collective-permute-done | bytes 131104 | tf_op jit(solution)/shard_map/ppermute | solution.py:203
  38.8 0.8 %shard_map.112 = f32[256,128]{1,0:T(8,128)} custom-call(f32[256,128]{1,0:T(8,128)S(1)} %get-tuple-element.9.a, f32[256,128]{1,0:T(8,128)S(1)} %collective-permute-done.7.b, f32[1,256]{1,0:T(1,128)S(1)} %dynamic-slice_add_fusion.t), custom_call_target="tpu_custom_call" | custom-call | tf_op jit(solution)/shard_map/pallas_call | solution.py:168
  (24 shorter events, 0.8 us)
Async XLA Ops:
  0.6 0.7 %copy-start.2 = (f32[16,256]{1,0:T(8,128)S(1)}, f32[16,256]{1,0:T(8,128)}, u32[]{:S(2)}) copy-start(f32[16,256]{1,0:T(8,128)} %refs_0_.1) | copy-start | bytes 49156
  1.4 0.9 %copy-start.4 = (f32[256,128]{1,0:T(8,128)S(1)}, f32[256,128]{1,0:T(8,128)}, u32[]{:S(2)}) copy-start(f32[256,128]{1,0:T(8,128)} %cotangent.1) | copy-start | bytes 393220
  2.3 0.9 %copy-start.5 = (s32[256,128]{1,0:T(8,128)S(1)}, s32[256,128]{1,0:T(8,128)}, u32[]{:S(2)}) copy-start(s32[256,128]{1,0:T(8,128)} %decision.1) | copy-start | bytes 393220
  3.3 7.8 %collective-permute-start = (f32[288,128]{1,0:T(8,128)S(1)}, f32[288,128]{1,0:T(8,128)S(1)}, u32[]{:S(2)}, u32[]{:S(2)}) collective-permute-start(f32[288,128]{1,0:T(8,128)S(1)} %shard_map.105.refs_3_), channel_id=1, source_target_pairs={{0,8},{2,10},{4,12},{6,14},{8,0},{10,2},{12,4},{14,6},{16,24},{18,... | collective-permute-start | bytes 442376 | tf_op jit(solution)/shard_map/ppermute | solution.py:203
  6.4 8.5 %collective-permute-start.1 = (f32[288,128]{1,0:T(8,128)S(1)}, f32[288,128]{1,0:T(8,128)S(1)}, u32[]{:S(2)}, u32[]{:S(2)}) collective-permute-start(f32[288,128]{1,0:T(8,128)S(1)} %shard_map.105.refs_3_), channel_id=1, source_target_pairs={{0,4},{2,6},{4,0},{6,2},{8,12},{10,14},{12,8},{14,10},{16,20},{18,... | collective-permute-start | bytes 442376 | tf_op jit(solution)/shard_map/ppermute | solution.py:203
  7.9 7.0 %collective-permute-start.2 = (f32[288,128]{1,0:T(8,128)S(1)}, f32[288,128]{1,0:T(8,128)S(1)}, u32[]{:S(2)}, u32[]{:S(2)}) collective-permute-start(f32[288,128]{1,0:T(8,128)S(1)} %shard_map.105.refs_3_), channel_id=1, source_target_pairs={{0,12},{2,14},{4,8},{6,10},{8,4},{10,6},{12,0},{14,2},{16,28},{18,... | collective-permute-start | bytes 442376 | tf_op jit(solution)/shard_map/ppermute | solution.py:203
  8.0 0.9 %copy-start.1 = (f32[16,4096]{1,0:T(8,128)S(1)}, f32[16,4096]{1,0:T(8,128)}, u32[]{:S(2)}) copy-start(f32[16,4096]{1,0:T(8,128)} %points.1) | copy-start | bytes 786436
  8.9 0.7 %copy-start.3 = (f32[16,256]{1,0:T(8,128)S(1)}, f32[16,256]{1,0:T(8,128)}, u32[]{:S(2)}) copy-start(f32[16,256]{1,0:T(8,128)} %refs_0_.1) | copy-start | bytes 49156
  9.6 0.7 %copy-start.8 = (f32[16]{0:T(128)S(1)}, f32[16]{0:T(128)}, u32[]{:S(2)}) copy-start(f32[16]{0:T(128)} %param.11) | copy-start | bytes 196
  16.6 8.6 %copy-start = (f32[4096,128]{1,0:T(8,128)S(1)}, f32[4096,128]{1,0:T(8,128)}, u32[]{:S(2)}) copy-start(f32[4096,128]{1,0:T(8,128)} %refs_5_.1) | copy-start | bytes 6291460
  16.6 13.8 %collective-permute-start.6 = (f32[2,256,128]{2,1,0:T(8,128)S(1)}, f32[2,256,128]{2,1,0:T(8,128)S(1)}, u32[]{:S(2)}, u32[]{:S(2)}) collective-permute-start(f32[2,256,128]{2,1,0:T(8,128)S(1)} %shard_map.111), channel_id=1, source_target_pairs={{0,2},{2,0},{4,6},{6,4},{8,10},{10,8},{12,14},{14,12},{16,18},{18,... | collective-permute-start | bytes 786440 | tf_op jit(solution)/shard_map/ppermute | solution.py:203
  18.9 1.4 %collective-permute-start.3 = (f32[1,4096]{1,0:T(1,128)S(1)}, f32[1,4096]{1,0:T(1,128)S(1)}, u32[]{:S(2)}, u32[]{:S(2)}) collective-permute-start(f32[1,4096]{1,0:T(1,128)S(1)} %shard_map.107), channel_id=1, source_target_pairs={{0,2},{2,0},{4,6},{6,4},{8,10},{10,8},{12,14},{14,12},{16,18},{18,... | collective-permute-start | bytes 49160 | tf_op jit(solution)/shard_map/ppermute | solution.py:203
  20.3 4.9 %collective-permute-start.4 = (f32[1,4096]{1,0:T(1,128)S(1)}, f32[1,4096]{1,0:T(1,128)S(1)}, u32[]{:S(2)}, u32[]{:S(2)}) collective-permute-start(f32[1,4096]{1,0:T(1,128)S(1)} %add.21.refs_3_), channel_id=1, source_target_pairs={{0,16},{2,18},{4,20},{6,22},{8,24},{10,26},{12,28},{14,30},{16,0},... | collective-permute-start | bytes 49160 | tf_op jit(solution)/shard_map/ppermute | solution.py:203
  24.6 9.2 %copy-start.6 = (f32[256,128]{1,0:T(8,128)S(1)}, f32[256,128]{1,0:T(8,128)}, u32[]{:S(2)}) copy-start(f32[256,128]{1,0:T(8,128)} %cash.1) | copy-start | bytes 393220
  24.6 9.2 %copy-start.7 = (f32[256,128]{1,0:T(8,128)S(1)}, f32[256,128]{1,0:T(8,128)}, u32[]{:S(2)}) copy-start(f32[256,128]{1,0:T(8,128)} %salvage.1) | copy-start | bytes 393220
  24.6 9.2 %copy-start.9 = (f32[128]{0:T(128)S(1)}, f32[128]{0:T(128)}, u32[]{:S(2)}) copy-start(f32[128]{0:T(128)} %param.15) | copy-start | bytes 1540
  28.8 5.0 %collective-permute-start.5 = (f32[256,128]{1,0:T(8,128)S(1)}, f32[256,128]{1,0:T(8,128)S(1)}, u32[]{:S(2)}, u32[]{:S(2)}) collective-permute-start(f32[256,128]{1,0:T(8,128)S(1)} %shard_map.108.own), channel_id=1, source_target_pairs={{0,1},{1,0},{2,3},{3,2},{4,5},{5,4},{6,7},{7,6},{8,9},{9,8},{10,11... | collective-permute-start | bytes 393224 | tf_op jit(solution)/shard_map/ppermute | solution.py:270
  30.4 8.5 %collective-permute-start.7 = (f32[256,128]{1,0:T(8,128)S(1)}, f32[256,128]{1,0:T(8,128)S(1)}, u32[]{:S(2)}, u32[]{:S(2)}) collective-permute-start(f32[256,128]{1,0:T(8,128)S(1)} %get-tuple-element.8), channel_id=1, source_target_pairs={{0,16},{2,18},{4,20},{6,22},{8,24},{10,26},{12,28},{14,30},{16,0},... | collective-permute-start | bytes 393224 | tf_op jit(solution)/shard_map/ppermute | solution.py:203

commit v3 on v2

v3 whole, which is shorter than its diff:
```python
import math

import jax
import jax.numpy as jnp
from jax import lax
from jax.experimental import pallas as pl
from jax.experimental.pallas import tpu as pltpu
from jax.sharding import PartitionSpec as P


LOG2E = math.log2(math.e)
F32 = jnp.float32
BF16 = jnp.bfloat16
GRANT = 16 * 2**20


def split2(x):
    hi = x.astype(BF16)
    return hi, (x - hi.astype(F32)).astype(BF16)


def split3(x):
    hi = x.astype(BF16)
    rest = x - hi.astype(F32)
    mid = rest.astype(BF16)
    return hi, mid, (rest - mid.astype(F32)).astype(BF16)


def dot(left, right, left_dim, right_dim):
    return lax.dot_general(left, right, (((left_dim,), (right_dim,)), ((), ())), preferred_element_type=F32)


def source_terms(mean, scale):
    scaled = mean * scale
    offset = -0.5 * jnp.sum(scaled * mean, axis=0, keepdims=True)
    s1, s2, s3 = split3(scaled)
    row = lax.broadcasted_iota(jnp.int32, scaled.shape, 0)
    o1, o2, o3 = (jnp.broadcast_to(o.astype(F32), scaled.shape) for o in split3(offset))
    tail = jnp.where(row == 0, o1, jnp.where(row == 1, o2, jnp.where(row == 2, o3, 0.0))).astype(BF16)
    return jnp.concatenate([s1, s1, s2, s2, s1, s3, tail], axis=0)


def target_terms(points):
    t1, t2, t3 = split3(points)
    row = lax.broadcasted_iota(jnp.int32, points.shape, 0)
    tail = jnp.where(row < 3, 1.0, 0.0).astype(BF16)
    return jnp.concatenate([t1, t2, t1, t2, t3, t1, tail], axis=0)


def swap_pairs(x):
    lane = lax.broadcasted_iota(jnp.int32, x.shape, 1)
    width = x.shape[1]
    return jnp.where(lane % 2 == 0, pltpu.roll(x, width - 1, 1), pltpu.roll(x, 1, 1))


def column(row):
    n = row.shape[1]
    wide = jnp.broadcast_to(row, (n, n))
    diagonal = lax.broadcasted_iota(jnp.int32, (n, n), 0) == lax.broadcasted_iota(jnp.int32, (n, n), 1)
    return jnp.sum(jnp.where(diagonal, wide, 0.0), axis=1, keepdims=True)


def load_kernel(cotangent, decision, mean, precision, points, adjoint_out, mean_out, precision_out, points_out, c, d, sems):
    pairs = ((cotangent, c), (decision, d), (points, points_out), (mean, mean_out), (precision, precision_out))
    copies = [pltpu.make_async_copy(src, dst, sems.at[i]) for i, (src, dst) in enumerate(pairs)]
    for copy in copies:
        copy.start()
    copies[0].wait()
    copies[1].wait()
    held = jnp.where(d[...] == 0, c[...], 0.0)
    moved = jnp.where(d[...] == 1, c[...], 0.0)
    adjoint_out[...] = held + swap_pairs(moved)
    for copy in copies[2:]:
        copy.wait()


def own_kernel(mean, precision, points, scale_out, terms_out, density_out, total_out):
    scale = column(precision[...]) * LOG2E
    scale_out[...] = jnp.broadcast_to(scale, scale_out.shape)
    left = source_terms(mean[...], scale)
    width = 256
    for j in range(points.shape[1] // width):
        cols = slice(j * width, (j + 1) * width)
        terms = target_terms(points[:, cols])
        terms_out[:, cols] = terms
        tile = jnp.exp2(dot(left, terms, 0, 0))
        density_out[:, cols] = tile
        total_out[:, cols] = jnp.sum(tile, axis=0, keepdims=True)


def total_kernel(scale, terms, total, *refs):
    means, out = refs[:-1], refs[-1]
    lefts = [source_terms(mean[...], scale[:, :1]) for mean in means]
    width = 256
    for j in range(terms.shape[1] // width):
        cols = slice(j * width, (j + 1) * width)
        tile = sum(jnp.exp2(dot(left, terms[:, cols], 0, 0)) for left in lefts)
        out[:, cols] = total[:, cols] + jnp.sum(tile, axis=0, keepdims=True)


def continuation_kernel(density, total, arrived, values, out, *, ratio):
    width = 256
    lanes = values.shape[1]
    acc = jnp.zeros((density.shape[0], 2 * lanes), F32)
    low = jnp.zeros((density.shape[0], lanes), F32)
    for j in range(density.shape[1] // width):
        cols = slice(j * width, (j + 1) * width)
        factor = ratio / (total[:, cols] + arrived[:, cols])
        hi, lo = split2(density[:, cols] * factor)
        vhi, vlo = split2(values[cols, :])
        acc += dot(hi, jnp.concatenate([vhi, vlo], axis=1), 1, 0)
        low += dot(lo, vhi, 1, 0)
    out[...] = acc[:, :lanes] + (acc[:, lanes:] + low)


def own_columns(mask, rows):
    return pl.multiple_of((lax.axis_index("src") ^ mask) * rows, 128) if rows % 128 == 0 else 0


def adjoint_kernel(scale, terms, *refs, mask):
    out = refs[-1]
    count = len(refs) // 2
    rows, lanes = out.shape
    left = terms[:, pl.ds(own_columns(mask, rows), rows)]
    acc = jnp.zeros((rows, 2 * lanes), F32)
    low = jnp.zeros((rows, lanes), F32)
    for mean, block in zip(refs[:count], refs[count:-1]):
        ahi, alo = split2(block[...])
        hi, lo = split2(jnp.exp2(dot(left, source_terms(mean[...], scale[:, :1]), 0, 0)))
        acc += dot(hi, jnp.concatenate([ahi, alo], axis=1), 1, 0)
        low += dot(lo, ahi, 1, 0)
    out[...] = acc[:, :lanes] + (acc[:, lanes:] + low)


def add_kernel(left, right, out):
    out[...] = left[...] + right[...]


def value_kernel(own, other, cash, salvage, cost, out):
    hold = own[...] + other[...] + cash[...]
    out[...] = jnp.maximum(jnp.maximum(hold, swap_pairs(hold) - cost[...]), salvage[...])


def finish_kernel(near, came, came_far, total, arrived, out, *, ratio):
    rows = out.shape[0]
    cols = pl.ds(own_columns(0, rows), rows)
    factor = column(ratio / (total[:, cols] + arrived[:, cols]))
    out[...] = (near[...] + came[...] + came_far[...]) * factor


def call(kernel, out_shape, *args, scratch=()):
    vmem = pl.BlockSpec(memory_space=pltpu.VMEM)
    specs, operands = [], []
    for a in args:
        if isinstance(a, Far):
            specs.append(pl.BlockSpec(memory_space=pltpu.HBM))
            operands.append(pltpu.with_memory_space_constraint(a.array, pltpu.HBM))
        else:
            specs.append(vmem)
            operands.append(pltpu.with_memory_space_constraint(a, pltpu.VMEM))
    return pl.pallas_call(
        kernel,
        out_shape=out_shape,
        in_specs=specs,
        out_specs=jax.tree.map(lambda _: vmem, out_shape),
        scratch_shapes=scratch,
        compiler_params=pltpu.CompilerParams(vmem_limit_bytes=GRANT),
    )(*operands)


class Far:
    def __init__(self, array):
        self.array = array


def shape(*dims, dtype=F32):
    return pltpu.VMEM(dims, dtype)


def result(*dims):
    return jax.ShapeDtypeStruct(dims, F32)


def on_device(source_mean, target_points, precision, target_values, cash, salvage, switch_cost, cotangent, decision):
    n = lax.axis_size("src")
    nt = lax.axis_size("tgt")
    factors, sources = source_mean.shape
    targets = target_points.shape[1]
    lanes = cash.shape[1]
    ratio = (sources * n) / (targets * nt)
    rows = targets // n
    top = n // 2

    def flip(x, mask):
        return lax.ppermute(x, "src", [(i, i ^ mask) for i in range(n)])

    def gather(x):
        blocks = [x]
        bit, level = 2, 0
        while bit < top:
            span = min(4, top // bit)
            payload = blocks[0] if len(blocks) == 1 else jnp.stack(blocks)
            more = [flip(payload, k * bit) for k in reversed(range(1, span))]
            more = [b for m in more for b in ([m] if len(blocks) == 1 else [m[i] for i in range(len(blocks))])]
            blocks = blocks + more
            bit *= span
            level += 1
        return blocks

    means = gather(source_mean)
    packed, mean, precision, points = call(
        load_kernel,
        (shape(sources, lanes), shape(factors, sources), shape(1, factors), shape(factors, targets)),
        Far(cotangent),
        Far(decision),
        Far(source_mean),
        Far(precision[None, :]),
        Far(target_points),
        scratch=(pltpu.VMEM((sources, lanes), F32), pltpu.VMEM((sources, lanes), jnp.int32), pltpu.SemaphoreType.DMA((5,))),
    )
    means[0] = mean
    packs = gather(packed)
    scale, terms, density, total = call(
        own_kernel,
        (shape(factors, lanes), shape(7 * factors, targets, dtype=BF16), shape(sources, targets), shape(1, targets)),
        mean,
        precision,
        points,
    )
    total = call(total_kernel, shape(1, targets), scale, terms, total, *means[1:])
    total = call(add_kernel, shape(1, targets), total, flip(total, 1))
    arrived = flip(total, top)

    def columns_of(x, mask):
        return x if rows % 128 == 0 else lax.dynamic_slice(x, (0, (lax.axis_index("src") ^ mask) * rows), (x.shape[0], rows))

    def adjoint(mask):
        def kernel(*refs):
            adjoint_kernel(*refs, mask=mask)

        return call(kernel, shape(rows, lanes), scale, columns_of(terms, mask), *means, *packs)

    came1 = flip(adjoint(1 ^ top), 1)
    far_half = call(add_kernel, shape(rows, lanes), adjoint(top), came1)
    came_far = flip(far_half, top)
    came0 = flip(adjoint(1), 1)
    near0 = adjoint(0)

    def finish(*refs):
        finish_kernel(*refs, ratio=ratio)

    target_adjoint = call(
        finish, result(rows, lanes), near0, came0, came_far, columns_of(total, 0), columns_of(arrived, 0)
    )

    def cont(*refs):
        continuation_kernel(*refs, ratio=ratio)

    mine = call(cont, shape(sources, lanes), density, total, arrived, target_values)
    theirs = mine
    for shift in range(1, nt):
        moved = lax.ppermute(mine, "tgt", [(i, (i + shift) % nt) for i in range(nt)])
        theirs = moved if shift == 1 else theirs + moved
    source_value = call(value_kernel, result(sources, lanes), mine, theirs, cash, salvage, switch_cost[None, :])
    return source_value, target_adjoint[None]


def solution(mesh):
    placed = (
        P(None, "src"),
        P(None, "tgt"),
        P(),
        P("tgt", None),
        P("src", None),
        P("src", None),
        P(),
        P("src", None),
        P("src", None),
    )

    return jax.shard_map(
        on_device,
        mesh=mesh,
        in_specs=placed,
        out_specs=(P("src", None), P("tgt", "src", None)),
        check_vma=False,
    )
```

time: 40 us -> 41.4 us (1.035)
  starting transfers between devices: 12 us -> 17.4 us
  local copies, waits for them, and re-layouts: 4.87 us -> 0.02 us
  waiting for transfers between devices: 10.3 us -> 12.4 us
  Pallas kernels: 11.7 us -> 10.7 us
    ppermute x7 -> x11, starting transfers between devices: 10.4 us -> 15.7 us  [flip(): return lax.ppermute(x, 'src', [(i, i ^ mask) for i in range(n)])]
    unnamed x20 -> x8, local copies, waits for them, and re-layouts: 4.87 us -> 0.02 us
    ppermute x7 -> x11, waiting for transfers between devices: 9.33 us -> 12.4 us  [flip(): return lax.ppermute(x, 'src', [(i, i ^ mask) for i in range(n)])]
    ppermute x1, waiting for transfers between devices: 0.95 us -> 0.01 us  [on_device(): lax.ppermute(mine, 'tgt', [(i, (i + shift) % nt) for i in range(nt)])]
    pallas_call x9 -> x12, Pallas kernels: 11.7 us -> 10.7 us  [call(): pl.pallas_call(kernel, out_shape=out_shape, in_specs=specs, out_specs=jax...]
  transfers between devices with their start and end apart: 8 -> 12, of which waited for: 5 -> 5; matrix products, arithmetic and copies ran while one was open for 0% -> 0% of each run, Pallas kernels for 23% -> 19%
where the time goes in v3:
time: 41.4 us; the launch traced here: 41.3 us
  starting transfers between devices  17.4 us (42%)
  waiting for transfers between devices  12.4 us (30%)
  Pallas kernels  10.7 us (26%)
  between operations  0.79 us (2%)
    ppermute x11, starting transfers between devices, flip(): return lax.ppermute(x, 'src', [(i, i ^ mask) for i in range(n)])  15.7 us
    ppermute x11, waiting for transfers between devices, flip(): return lax.ppermute(x, 'src', [(i, i ^ mask) for i in range(n)])  12.4 us
    pallas_call x12, Pallas kernels, call(): pl.pallas_call(kernel, out_shape=out_shape, in_specs=specs, out_specs=jax...  10.7 us
    ppermute x1, starting transfers between devices, on_device(): lax.ppermute(mine, 'tgt', [(i, (i + shift) % nt) for i in range(nt)])  1.66 us
  transfers between devices with their start and end apart: 12, of which 5 were waited for; matrix products, arithmetic and copies ran while one was open for 0% of the time, Pallas kernels for 19%

profile of v3, /device:TPU:0, one launch (start us, length us, event | category | flops | bytes accessed | tf_op | source)
XLA Modules:
  0.0 41.3 jit_solution(11986116688846484897)
XLA Ops:
  0.6 1.3 %shard_map.104 = (f32[256,128]{1,0:T(8,128)S(1)}, f32[16,256]{1,0:T(8,128)S(1)}, f32[1,16]{1,0:T(1,128)S(1)}, f32[16,4096]{1,0:T(8,128)S(1)}) custom-call(f32[256,128]{1,0:T(8,128)} %cotangent.1, s32[256,128]{1,0:T(8,128)} %decision.1, f32[16,256]{1,0:T(8,128)} %mean.1, f32[1,16]{1,0:T(1,128)} %bitcast.5, f32[16,4096]{1,0:T(8,128)} %points.1), custom_call_target="tpu_custom_call" | custom-call | tf_op jit(solution)/shard_map/pallas_call | solution.py:161
  2.0 4.1 %collective-permute-start.6 = (f32[256,128]{1,0:T(8,128)S(1)}, f32[256,128]{1,0:T(8,128)S(1)}, u32[]{:S(2)}, u32[]{:S(2)}) collective-permute-start(f32[256,128]{1,0:T(8,128)S(1)} %get-tuple-element.17.refs_6_), channel_id=1, source_target_pairs={{0,12},{2,14},{4,8},{6,10},{8,4},{10,6},{12,0},{14,2},{16,28},{18,... | collective-permute-start | bytes 393224 | tf_op jit(solution)/shard_map/ppermute | solution.py:195
  6.0 0.4 %collective-permute-start.7 = (f32[256,128]{1,0:T(8,128)S(1)}, f32[256,128]{1,0:T(8,128)S(1)}, u32[]{:S(2)}, u32[]{:S(2)}) collective-permute-start(f32[256,128]{1,0:T(8,128)S(1)} %get-tuple-element.17.refs_6_), channel_id=1, source_target_pairs={{0,8},{2,10},{4,12},{6,14},{8,0},{10,2},{12,4},{14,6},{16,24},{18,... | collective-permute-start | bytes 393224 | tf_op jit(solution)/shard_map/ppermute | solution.py:195
  6.7 2.8 %collective-permute-start = (f32[16,256]{1,0:T(8,128)}, f32[16,256]{1,0:T(8,128)S(1)}, u32[]{:S(2)}, u32[]{:S(2)}) collective-permute-start(f32[16,256]{1,0:T(8,128)} %mean.1), channel_id=1, source_target_pairs={{0,12},{2,14},{4,8},{6,10},{8,4},{10,6},{12,0},{14,2},{16,28},{18,... | collective-permute-start | bytes 49160 | tf_op jit(solution)/shard_map/ppermute | solution.py:195
  9.5 0.4 %collective-permute-start.1 = (f32[16,256]{1,0:T(8,128)}, f32[16,256]{1,0:T(8,128)S(1)}, u32[]{:S(2)}, u32[]{:S(2)}) collective-permute-start(f32[16,256]{1,0:T(8,128)} %mean.1), channel_id=1, source_target_pairs={{0,8},{2,10},{4,12},{6,14},{8,0},{10,2},{12,4},{14,6},{16,24},{18,... | collective-permute-start | bytes 49160 | tf_op jit(solution)/shard_map/ppermute | solution.py:195
  10.0 2.9 %collective-permute-done.refs_0_.refs_3_ = f32[16,256]{1,0:T(8,128)S(1)} collective-permute-done((f32[16,256]{1,0:T(8,128)}, f32[16,256]{1,0:T(8,128)S(1)}, u32[]{:S(2)}, u32[]{:S(2)}) %collective-permute-start) | collective-permute-done | bytes 16416 | tf_op jit(solution)/shard_map/ppermute | solution.py:195
  12.9 1.6 %collective-permute-start.2 = (f32[16,256]{1,0:T(8,128)}, f32[16,256]{1,0:T(8,128)S(1)}, u32[]{:S(2)}, u32[]{:S(2)}) collective-permute-start(f32[16,256]{1,0:T(8,128)} %mean.1), channel_id=1, source_target_pairs={{0,4},{2,6},{4,0},{6,2},{8,12},{10,14},{12,8},{14,10},{16,20},{18,... | collective-permute-start | bytes 49160 | tf_op jit(solution)/shard_map/ppermute | solution.py:195
  14.5 0.8 %shard_map.105 = (f32[16,128]{1,0:T(8,128)S(1)}, bf16[112,4096]{1,0:T(8,128)(2,1)S(1)}, f32[256,4096]{1,0:T(8,128)S(1)}, f32[1,4096]{1,0:T(1,128)S(1)}) custom-call(f32[16,256]{1,0:T(8,128)S(1)} %get-tuple-element.10.mean.refs_2_, f32[1,16]{1,0:T(1,128)S(1)} %get-tuple-element.11.precision, f32[16,4096]{1,0:T(8,128)S(1)} %get-tuple-element.12.points), custom_call_target="tpu_custom_call" | custom-call | tf_op jit(solution)/shard_map/pallas_call | solution.py:161
  15.3 1.5 %collective-permute-done.2.refs_2_.refs_5_ = f32[16,256]{1,0:T(8,128)S(1)} collective-permute-done((f32[16,256]{1,0:T(8,128)}, f32[16,256]{1,0:T(8,128)S(1)}, u32[]{:S(2)}, u32[]{:S(2)}) %collective-permute-start.2) | collective-permute-done | bytes 16416 | tf_op jit(solution)/shard_map/ppermute | solution.py:195
  16.8 0.9 %shard_map.113 = f32[256,128]{1,0:T(8,128)S(1)} custom-call(f32[16,128]{1,0:T(8,128)S(1)} %get-tuple-element.14.scale.refs_0_, bf16[112,4096]{1,0:T(8,128)(2,1)S(1)} %get-tuple-element.15.terms.refs_1_, f32[16,256]{1,0:T(8,128)S(1)} %get-tuple-element.10.mean.refs_2_, f32[16,256]{1,0:T(8,128)S(1)} %collective-permute-done.refs_0_.refs_3_, ...), custom_call_target="tpu_custom_call" | custom-call | tf_op jit(solution)/shard_map/pallas_call | solution.py:161
  17.8 2.0 %shard_map.106.left = f32[1,4096]{1,0:T(1,128)S(1)} custom-call(f32[16,128]{1,0:T(8,128)S(1)} %get-tuple-element.14.scale.refs_0_, bf16[112,4096]{1,0:T(8,128)(2,1)S(1)} %get-tuple-element.15.terms.refs_1_, f32[1,4096]{1,0:T(1,128)S(1)} %get-tuple-element.16.total, f32[16,256]{1,0:T(8,128)S(1)} %collective-permute-done.refs_0_.refs_3_, ...), custom_call_target="tpu_custom_call" | custom-call | tf_op jit(solution)/shard_map/pallas_call | solution.py:161
  19.8 0.6 %collective-permute-start.3 = (f32[1,4096]{1,0:T(1,128)S(1)}, f32[1,4096]{1,0:T(1,128)S(1)}, u32[]{:S(2)}, u32[]{:S(2)}) collective-permute-start(f32[1,4096]{1,0:T(1,128)S(1)} %shard_map.106.left), channel_id=1, source_target_pairs={{0,2},{2,0},{4,6},{6,4},{8,10},{10,8},{12,14},{14,12},{16,18},{18,... | collective-permute-start | bytes 49160 | tf_op jit(solution)/shard_map/ppermute | solution.py:195
  20.4 0.8 %collective-permute-done.3.right = f32[1,4096]{1,0:T(1,128)S(1)} collective-permute-done((f32[1,4096]{1,0:T(1,128)S(1)}, f32[1,4096]{1,0:T(1,128)S(1)}, u32[]{:S(2)}, u32[]{:S(2)}) %collective-permute-start.3) | collective-permute-done | bytes 16416 | tf_op jit(solution)/shard_map/ppermute | solution.py:195
  21.2 2.7 %collective-permute-start.4 = (f32[1,4096]{1,0:T(1,128)S(1)}, f32[1,4096]{1,0:T(1,128)S(1)}, u32[]{:S(2)}, u32[]{:S(2)}) collective-permute-start(f32[1,4096]{1,0:T(1,128)S(1)} %shard_map.107.refs_1_.refs_3_), channel_id=1, source_target_pairs={{0,16},{2,18},{4,20},{6,22},{8,24},{10,26},{12,28},{14,30},{16,0},... | collective-permute-start | bytes 49160 | tf_op jit(solution)/shard_map/ppermute | solution.py:195
  23.9 1.9 %collective-permute-done.4.refs_2_.refs_4_ = f32[1,4096]{1,0:T(1,128)S(1)} collective-permute-done((f32[1,4096]{1,0:T(1,128)S(1)}, f32[1,4096]{1,0:T(1,128)S(1)}, u32[]{:S(2)}, u32[]{:S(2)}) %collective-permute-start.4) | collective-permute-done | bytes 16416 | tf_op jit(solution)/shard_map/ppermute | solution.py:195
  25.8 1.3 %shard_map.108.own = f32[256,128]{1,0:T(8,128)S(1)} custom-call(f32[256,4096]{1,0:T(8,128)S(1)} %get-tuple-element.13.refs_0_, f32[1,4096]{1,0:T(1,128)S(1)} %shard_map.107.refs_1_.refs_3_, f32[1,4096]{1,0:T(1,128)S(1)} %collective-permute-done.4.refs_2_.refs_4_, f32[4096,128]{1,0:T(8,128)S(1)} %copy-done), custom_call_target="tpu_custom_call" | custom-call | tf_op jit(solution)/shard_map/pallas_call | solution.py:161
  27.2 1.7 %collective-permute-start.5 = (f32[256,128]{1,0:T(8,128)S(1)}, f32[256,128]{1,0:T(8,128)S(1)}, u32[]{:S(2)}, u32[]{:S(2)}) collective-permute-start(f32[256,128]{1,0:T(8,128)S(1)} %shard_map.108.own), channel_id=1, source_target_pairs={{0,1},{1,0},{2,3},{3,2},{4,5},{5,4},{6,7},{7,6},{8,9},{9,8},{10,11... | collective-permute-start | bytes 393224 | tf_op jit(solution)/shard_map/ppermute | solution.py:262
  28.8 0.9 %shard_map.111 = f32[256,128]{1,0:T(8,128)S(1)} custom-call(f32[16,128]{1,0:T(8,128)S(1)} %get-tuple-element.14.scale.refs_0_, bf16[112,4096]{1,0:T(8,128)(2,1)S(1)} %get-tuple-element.15.terms.refs_1_, f32[16,256]{1,0:T(8,128)S(1)} %get-tuple-element.10.mean.refs_2_, f32[16,256]{1,0:T(8,128)S(1)} %collective-permute-done.refs_0_.refs_3_, ...), custom_call_target="tpu_custom_call" | custom-call | tf_op jit(solution)/shard_map/pallas_call | solution.py:161
  29.9 0.9 %shard_map.112.left = f32[256,128]{1,0:T(8,128)S(1)} custom-call(f32[16,128]{1,0:T(8,128)S(1)} %get-tuple-element.14.scale.refs_0_, bf16[112,4096]{1,0:T(8,128)(2,1)S(1)} %get-tuple-element.15.terms.refs_1_, f32[16,256]{1,0:T(8,128)S(1)} %get-tuple-element.10.mean.refs_2_, f32[16,256]{1,0:T(8,128)S(1)} %collective-permute-done.refs_0_.refs_3_, ...), custom_call_target="tpu_custom_call" | custom-call | tf_op jit(solution)/shard_map/pallas_call | solution.py:161
  30.8 2.7 %collective-permute-start.11 = (f32[256,128]{1,0:T(8,128)S(1)}, f32[256,128]{1,0:T(8,128)S(1)}, u32[]{:S(2)}, u32[]{:S(2)}) collective-permute-start(f32[256,128]{1,0:T(8,128)S(1)} %shard_map.114), channel_id=1, source_target_pairs={{0,16},{2,18},{4,20},{6,22},{8,24},{10,26},{12,28},{14,30},{16,0},... | collective-permute-start | bytes 393224 | tf_op jit(solution)/shard_map/ppermute | solution.py:195
  33.5 0.9 %shard_map.110.refs_0_ = f32[256,128]{1,0:T(8,128)S(1)} custom-call(f32[16,128]{1,0:T(8,128)S(1)} %get-tuple-element.14.scale.refs_0_, bf16[112,4096]{1,0:T(8,128)(2,1)S(1)} %get-tuple-element.15.terms.refs_1_, f32[16,256]{1,0:T(8,128)S(1)} %get-tuple-element.10.mean.refs_2_, f32[16,256]{1,0:T(8,128)S(1)} %collective-permute-done.refs_0_.refs_3_, ...), custom_call_target="tpu_custom_call" | custom-call | tf_op jit(solution)/shard_map/pallas_call | solution.py:161
  34.5 0.8 %shard_map.109 = f32[256,128]{1,0:T(8,128)} custom-call(f32[256,128]{1,0:T(8,128)S(1)} %shard_map.108.own, f32[256,128]{1,0:T(8,128)S(1)} %collective-permute-done.5.other, f32[256,128]{1,0:T(8,128)S(1)} %copy-done.1, f32[256,128]{1,0:T(8,128)S(1)} %copy-done.2, f32[1,128]{1,0:T(1,128)S(1)} %bitcast.3), custom_call_target="tpu_custom_call" | custom-call | tf_op jit(solution)/shard_map/pallas_call | solution.py:161
  35.3 5.2 %collective-permute-done.11.refs_2_ = f32[256,128]{1,0:T(8,128)S(1)} collective-permute-done((f32[256,128]{1,0:T(8,128)S(1)}, f32[256,128]{1,0:T(8,128)S(1)}, u32[]{:S(2)}, u32[]{:S(2)}) %collective-permute-start.11) | collective-permute-done | bytes 131104 | tf_op jit(solution)/shard_map/ppermute | solution.py:195
  40.5 0.8 %shard_map.115 = f32[256,128]{1,0:T(8,128)} custom-call(f32[256,128]{1,0:T(8,128)S(1)} %shard_map.110.refs_0_, f32[256,128]{1,0:T(8,128)S(1)} %collective-permute-done.9.refs_1_, f32[256,128]{1,0:T(8,128)S(1)} %collective-permute-done.11.refs_2_, f32[1,4096]{1,0:T(1,128)S(1)} %shard_map.107.refs_1_.refs_3_, f32[1,4096]{1,0:T(1,128)S(1)} %collective-permute-done.4.refs_2_.refs_4_), custom_call_target="tpu_custom_call" | custom-call | tf_op jit(solution)/shard_map/pallas_call | solution.py:161
  (20 shorter events, 0.4 us)
Async XLA Ops:
  0.6 25.2 %copy-start = (f32[4096,128]{1,0:T(8,128)S(1)}, f32[4096,128]{1,0:T(8,128)}, u32[]{:S(2)}) copy-start(f32[4096,128]{1,0:T(8,128)} %refs_3_.1) | copy-start | bytes 6291460
  2.0 14.9 %collective-permute-start.6 = (f32[256,128]{1,0:T(8,128)S(1)}, f32[256,128]{1,0:T(8,128)S(1)}, u32[]{:S(2)}, u32[]{:S(2)}) collective-permute-start(f32[256,128]{1,0:T(8,128)S(1)} %get-tuple-element.17.refs_6_), channel_id=1, source_target_pairs={{0,12},{2,14},{4,8},{6,10},{8,4},{10,6},{12,0},{14,2},{16,28},{18,... | collective-permute-start | bytes 393224 | tf_op jit(solution)/shard_map/ppermute | solution.py:195
  6.0 10.8 %collective-permute-start.7 = (f32[256,128]{1,0:T(8,128)S(1)}, f32[256,128]{1,0:T(8,128)S(1)}, u32[]{:S(2)}, u32[]{:S(2)}) collective-permute-start(f32[256,128]{1,0:T(8,128)S(1)} %get-tuple-element.17.refs_6_), channel_id=1, source_target_pairs={{0,8},{2,10},{4,12},{6,14},{8,0},{10,2},{12,4},{14,6},{16,24},{18,... | collective-permute-start | bytes 393224 | tf_op jit(solution)/shard_map/ppermute | solution.py:195
  6.5 10.3 %collective-permute-start.8 = (f32[256,128]{1,0:T(8,128)S(1)}, f32[256,128]{1,0:T(8,128)S(1)}, u32[]{:S(2)}, u32[]{:S(2)}) collective-permute-start(f32[256,128]{1,0:T(8,128)S(1)} %get-tuple-element.17.refs_6_), channel_id=1, source_target_pairs={{0,4},{2,6},{4,0},{6,2},{8,12},{10,14},{12,8},{14,10},{16,20},{18,... | collective-permute-start | bytes 393224 | tf_op jit(solution)/shard_map/ppermute | solution.py:195
  6.7 6.2 %collective-permute-start = (f32[16,256]{1,0:T(8,128)}, f32[16,256]{1,0:T(8,128)S(1)}, u32[]{:S(2)}, u32[]{:S(2)}) collective-permute-start(f32[16,256]{1,0:T(8,128)} %mean.1), channel_id=1, source_target_pairs={{0,12},{2,14},{4,8},{6,10},{8,4},{10,6},{12,0},{14,2},{16,28},{18,... | collective-permute-start | bytes 49160 | tf_op jit(solution)/shard_map/ppermute | solution.py:195
  9.5 5.8 %collective-permute-start.1 = (f32[16,256]{1,0:T(8,128)}, f32[16,256]{1,0:T(8,128)S(1)}, u32[]{:S(2)}, u32[]{:S(2)}) collective-permute-start(f32[16,256]{1,0:T(8,128)} %mean.1), channel_id=1, source_target_pairs={{0,8},{2,10},{4,12},{6,14},{8,0},{10,2},{12,4},{14,6},{16,24},{18,... | collective-permute-start | bytes 49160 | tf_op jit(solution)/shard_map/ppermute | solution.py:195
  12.9 3.9 %collective-permute-start.2 = (f32[16,256]{1,0:T(8,128)}, f32[16,256]{1,0:T(8,128)S(1)}, u32[]{:S(2)}, u32[]{:S(2)}) collective-permute-start(f32[16,256]{1,0:T(8,128)} %mean.1), channel_id=1, source_target_pairs={{0,4},{2,6},{4,0},{6,2},{8,12},{10,14},{12,8},{14,10},{16,20},{18,... | collective-permute-start | bytes 49160 | tf_op jit(solution)/shard_map/ppermute | solution.py:195
  17.8 13.0 %collective-permute-start.10 = (f32[256,128]{1,0:T(8,128)S(1)}, f32[256,128]{1,0:T(8,128)S(1)}, u32[]{:S(2)}, u32[]{:S(2)}) collective-permute-start(f32[256,128]{1,0:T(8,128)S(1)} %shard_map.113), channel_id=1, source_target_pairs={{0,2},{2,0},{4,6},{6,4},{8,10},{10,8},{12,14},{14,12},{16,18},{18,... | collective-permute-start | bytes 393224 | tf_op jit(solution)/shard_map/ppermute | solution.py:195
  19.8 1.4 %collective-permute-start.3 = (f32[1,4096]{1,0:T(1,128)S(1)}, f32[1,4096]{1,0:T(1,128)S(1)}, u32[]{:S(2)}, u32[]{:S(2)}) collective-permute-start(f32[1,4096]{1,0:T(1,128)S(1)} %shard_map.106.left), channel_id=1, source_target_pairs={{0,2},{2,0},{4,6},{6,4},{8,10},{10,8},{12,14},{14,12},{16,18},{18,... | collective-permute-start | bytes 49160 | tf_op jit(solution)/shard_map/ppermute | solution.py:195
  21.2 4.6 %collective-permute-start.4 = (f32[1,4096]{1,0:T(1,128)S(1)}, f32[1,4096]{1,0:T(1,128)S(1)}, u32[]{:S(2)}, u32[]{:S(2)}) collective-permute-start(f32[1,4096]{1,0:T(1,128)S(1)} %shard_map.107.refs_1_.refs_3_), channel_id=1, source_target_pairs={{0,16},{2,18},{4,20},{6,22},{8,24},{10,26},{12,28},{14,30},{16,0},... | collective-permute-start | bytes 49160 | tf_op jit(solution)/shard_map/ppermute | solution.py:195
  27.1 7.3 %copy-start.1 = (f32[256,128]{1,0:T(8,128)S(1)}, f32[256,128]{1,0:T(8,128)}, u32[]{:S(2)}) copy-start(f32[256,128]{1,0:T(8,128)} %cash.1) | copy-start | bytes 393220
  27.1 7.3 %copy-start.2 = (f32[256,128]{1,0:T(8,128)S(1)}, f32[256,128]{1,0:T(8,128)}, u32[]{:S(2)}) copy-start(f32[256,128]{1,0:T(8,128)} %salvage.1) | copy-start | bytes 393220
  27.2 7.3 %copy-start.3 = (f32[128]{0:T(128)S(1)}, f32[128]{0:T(128)}, u32[]{:S(2)}) copy-start(f32[128]{0:T(128)} %param.15) | copy-start | bytes 1540
  27.2 7.3 %collective-permute-start.5 = (f32[256,128]{1,0:T(8,128)S(1)}, f32[256,128]{1,0:T(8,128)S(1)}, u32[]{:S(2)}, u32[]{:S(2)}) collective-permute-start(f32[256,128]{1,0:T(8,128)S(1)} %shard_map.108.own), channel_id=1, source_target_pairs={{0,1},{1,0},{2,3},{3,2},{4,5},{5,4},{6,7},{7,6},{8,9},{9,8},{10,11... | collective-permute-start | bytes 393224 | tf_op jit(solution)/shard_map/ppermute | solution.py:262
  29.8 5.5 %collective-permute-start.9 = (f32[256,128]{1,0:T(8,128)S(1)}, f32[256,128]{1,0:T(8,128)S(1)}, u32[]{:S(2)}, u32[]{:S(2)}) collective-permute-start(f32[256,128]{1,0:T(8,128)S(1)} %shard_map.111), channel_id=1, source_target_pairs={{0,2},{2,0},{4,6},{6,4},{8,10},{10,8},{12,14},{14,12},{16,18},{18,... | collective-permute-start | bytes 393224 | tf_op jit(solution)/shard_map/ppermute | solution.py:195
  30.8 9.7 %collective-permute-start.11 = (f32[256,128]{1,0:T(8,128)S(1)}, f32[256,128]{1,0:T(8,128)S(1)}, u32[]{:S(2)}, u32[]{:S(2)}) collective-permute-start(f32[256,128]{1,0:T(8,128)S(1)} %shard_map.114), channel_id=1, source_target_pairs={{0,16},{2,18},{4,20},{6,22},{8,24},{10,26},{12,28},{14,30},{16,0},... | collective-permute-start | bytes 393224 | tf_op jit(solution)/shard_map/ppermute | solution.py:195
